TPU v7x, 32 devices: a whole 2x2x4 slice. The times are simulated.
32 devices in a mesh: fault: 16 (over z, x, core), rup: 2 (over y).
Axes of the slice: x: 2, y: 2, z: 4, core: 2. Of those that a mesh axis runs over, the one named last changes fastest.
Arguments:
- green: bfloat16 [32, 128, 6, 2, 2, 1024], P('fault', None, None, None, None, 'rup'), may hold values from -6 to 6
- slip_weights: bfloat16 [256, 16, 128, 6], P(('fault', 'rup')), may hold values from -0.0546875 to 0.0546875
- slip_spectra: bfloat16 [256, 16, 2, 1024], P(('fault', 'rup')), may hold values from -6 to 6
- block_lists: int32 [256, 16], P(('fault', 'rup')), may hold values from 0 to 31, all different within a row; in each aligned block of 16 rows (0 to 15, 16 to 31, ...) at most 12 rows name the same one
- block_counts: int32 [256], P(('fault', 'rup')), may hold values from 1 to 16, 3072 in all
- natural_freq: float32 [64], replicated, may hold values from 0.02 to 0.8
- damping: float32 [64], replicated, may hold values from 0.03 to 0.3
Outputs:
- waveforms: float32 [256, 2, 2048], P(('fault', 'rup'))
- osc_spectra: float32 [256, 2, 64], P(('fault', 'rup'))
Inputs may be any that keep to these rules, and one draw needn't show every extreme that they name: `block_lists`: the 16 blocks of one rupture are distinct. In each aligned run of 16 ruptures no block is named by more than 12 slots, active or not, and some block is named by exactly 12. `block_counts`: the counts of all ruptures sum to 3072; some rupture has 16.
All inputs are finite; a program needn't handle non-finite values. No bound on the sum of `block_counts` on one device may be relied on, other than what follows from the above.
Results may differ from a plain program's by a relative error of at most 0.0037.
Values may be sent and summed in bfloat16 or wider, within the bound.
A program may use at most 64 MiB of HBM per device.

v0:
```python
import math

import jax
import jax.numpy as jnp
from jax import lax
from jax.sharding import PartitionSpec as P


def inverse_table(freq_count):
    sample_count = 2 * freq_count
    freq_index = jnp.arange(freq_count, dtype=jnp.int32)
    time_index = jnp.arange(sample_count, dtype=jnp.int32)
    phase_index = freq_index[:, None] * time_index[None, :] % sample_count
    phase_angle = phase_index.astype(jnp.float32) * jnp.float32(2.0 * math.pi / sample_count)
    norm_scale = jnp.float32(1.0 / math.sqrt(freq_count))
    cosines = jnp.cos(phase_angle) * norm_scale
    sines = -jnp.sin(phase_angle) * norm_scale
    return jnp.concatenate([cosines, sines], axis=0).astype(jnp.bfloat16)


def oscillator_gain(natural_freq, damping, freq_count):
    omega_f = jnp.arange(freq_count, dtype=jnp.float32) * jnp.float32(math.pi / freq_count)
    omega_nat = jnp.float32(math.pi) * natural_freq[:, None]
    stiffness = omega_nat * omega_nat
    den_real = stiffness - omega_f[None, :] * omega_f[None, :]
    den_imag = 2.0 * damping[:, None] * omega_nat * omega_f[None, :]
    magnitude = den_real * den_real + den_imag * den_imag
    return (stiffness * den_real / magnitude, -stiffness * den_imag / magnitude)


def oscillate(spectra, gain_real, gain_imag, dft_table):
    rupture_count = spectra.shape[0]
    comp_count = spectra.shape[1]
    freq_count = spectra.shape[3]
    period_count = gain_real.shape[0]
    spec_real = spectra[:, :, 0][:, :, None, :]
    spec_imag = spectra[:, :, 1][:, :, None, :]
    resp_real = gain_real * spec_real - gain_imag * spec_imag
    resp_imag = gain_real * spec_imag + gain_imag * spec_real
    resp_rows = jnp.concatenate([resp_real, resp_imag], axis=3).astype(jnp.bfloat16)
    resp_rows = resp_rows.reshape(rupture_count * comp_count * period_count, 2 * freq_count)
    wave_rows = spectra.reshape(rupture_count * comp_count, 2 * freq_count).astype(jnp.bfloat16)
    stacked = jnp.concatenate([resp_rows, wave_rows], axis=0)
    outcome = jnp.dot(stacked, dft_table, preferred_element_type=jnp.float32)
    split_at = rupture_count * comp_count * period_count
    peaks = jnp.max(jnp.abs(outcome[:split_at]), axis=1).reshape(
        rupture_count, comp_count, period_count
    )
    waveform = outcome[split_at:].reshape(rupture_count, comp_count, 2 * freq_count)
    return (waveform, peaks)


def complex_times(prod_real, prod_imag, slip_real, slip_imag):
    return (
        prod_real * slip_real - prod_imag * slip_imag,
        prod_real * slip_imag + prod_imag * slip_real,
    )


def body(green, slip_weights, slip_spectra, block_lists, block_counts, natural_freq, damping):
    fault_count = lax.axis_size("fault")
    group_size = lax.axis_size("rup")
    owned_count, slot_width = block_lists.shape
    blocks_local = green.shape[0]
    comp_count = green.shape[3]
    freq_local = green.shape[5]
    inner_width = slip_weights.shape[2] * slip_weights.shape[3]
    freq_count = slip_spectra.shape[3]
    block_total = blocks_local * fault_count
    row_count = group_size * owned_count * slot_width
    capacity = max(2, (3 * row_count + 2 * block_total - 1) // (2 * block_total))
    slot_count = block_total * capacity
    group_weights, group_blocks, group_counts = (
        lax.all_gather(slip_weights, "rup", axis=0, tiled=True),
        lax.all_gather(block_lists, "rup", axis=0, tiled=True),
        lax.all_gather(block_counts, "rup", axis=0, tiled=True),
    )
    flat_blocks = group_blocks.reshape(row_count)
    slot_index = lax.broadcasted_iota(jnp.int32, (group_size * owned_count, slot_width), 1)
    is_live = (slot_index < group_counts[:, None]).reshape(row_count)
    block_ids = jnp.arange(block_total, dtype=jnp.int32)
    hit_table = ((flat_blocks[:, None] == block_ids[None, :]) & is_live[:, None]).astype(jnp.int32)
    rank_in = jnp.sum(jnp.cumsum(hit_table, axis=0) * hit_table, axis=1) - 1
    target = jnp.where(is_live, flat_blocks * capacity + rank_in, slot_count)
    fetch_at = jnp.minimum(target, slot_count - 1)
    values = group_weights.reshape(row_count, inner_width)
    blanks = jnp.zeros((slot_count,) + values.shape[1:], values.dtype)
    filled = blanks.at[target].set(values, mode="drop")
    weight_send = filled.reshape((fault_count, blocks_local, capacity) + values.shape[1:])
    slip_group = lax.all_to_all(slip_spectra, "rup", split_axis=3, concat_axis=0, tiled=True)
    slip_rows = slip_group.reshape(row_count, 2 * freq_local)
    tile_mats = green.reshape(blocks_local, inner_width, comp_count * 2 * freq_local)
    product = jnp.einsum(
        "sbci,bix->sbcx",
        lax.all_to_all(weight_send, "fault", split_axis=0, concat_axis=0, tiled=True),
        tile_mats,
        preferred_element_type=jnp.float32,
    )
    returned = lax.all_to_all(
        product.reshape(product.shape[:3] + (comp_count, 2, freq_local)),
        "fault",
        split_axis=0,
        concat_axis=0,
        tiled=True,
    )
    picked = returned.reshape(slot_count, comp_count, 2, freq_local)[fetch_at]
    slip_f = slip_rows.astype(jnp.float32).reshape(row_count, 1, 2, freq_local)
    real_part, imag_part = complex_times(
        picked[:, :, 0], picked[:, :, 1], slip_f[:, :, 0], slip_f[:, :, 1]
    )
    term_rows = jnp.where(
        is_live[:, None, None, None], jnp.stack([real_part, imag_part], axis=2), jnp.float32(0.0)
    )
    summed = jnp.sum(
        term_rows.reshape(group_size * owned_count, slot_width, comp_count, 2, freq_local), axis=1
    )
    spectra = lax.all_to_all(summed, "rup", split_axis=0, concat_axis=3, tiled=True)
    gain_real, gain_imag = oscillator_gain(natural_freq, damping, freq_count)
    dft_table = inverse_table(freq_count)
    waveform, peaks = oscillate(spectra, gain_real, gain_imag, dft_table)
    return (waveform, peaks)


def solution(mesh):
    return jax.shard_map(
        body,
        mesh=mesh,
        in_specs=(
            P("fault", None, None, None, None, "rup"),
            P(("fault", "rup"), None, None, None),
            P(("fault", "rup"), None, None, None),
            P(("fault", "rup"), None),
            P(("fault", "rup")),
            P(),
            P(),
        ),
        out_specs=(P(("fault", "rup"), None, None), P(("fault", "rup"), None, None)),
        check_vma=False,
    )
```

profile of v0, /device:TPU:10, one launch (start us, length us, event | category | flops | bytes accessed | tf_op | source)
XLA Modules:
  0.0 192.6 jit_solution(2906720177345622297)
XLA Ops:
  0.6 1.2 dynamic-slice
  2.5 0.9 dynamic-update-slice
  3.4 4.3 %all-reduce = s32[16]{0:T(128)S(1)} all-reduce(s32[16]{0:T(128)S(1)} %dynamic-update-slice), channel_id=1, replica_groups=mesh['fault'=16,'rup'=2] {'rup'}, use_global_device_ids=true, to_apply=%add | all-reduce | flops 16 | bytes 128
  8.0 4.5 %all_gather.10 = s32[16,16]{1,0:T(8,128)S(1)} all-gather(s32[8,16]{1,0:T(8,128)} %param.10), channel_id=1, replica_groups=mesh['fault'=16,'rup'=2] {'rup'}, dimensions={0}, use_global_device_ids=true | all-gather | bytes 1536 | tf_op jit(solution)/shard_map/all_gather | solution.py:75
  13.9 6.5 %all_gather.11 = bf16[16,16,128,6]{2,1,3,0:T(8,128)(2,1)S(1)} all-gather(bf16[8,16,128,6]{2,1,3,0:T(8,128)(2,1)} %param.8), channel_id=1, replica_groups=mesh['fault'=16,'rup'=2] {'rup'}, dimensions={0}, use_global_device_ids=true | all-gather | bytes 589824 | tf_op jit(solution)/shard_map/all_gather | solution.py:74
  20.5 4.4 %copy.50 = bf16[16,16,128,6]{1,0,3,2:T(8,128)(2,1)S(1)} copy(bf16[16,16,128,6]{2,1,3,0:T(8,128)(2,1)S(1)} %all_gather.11) | data formatting | bytes 786432 | tf_op jit(solution)/shard_map/all_gather | solution.py:74
  24.8 3.0 %reshape.366 = bf16[256,768]{0,1:T(8,128)(2,1)S(1)} reshape(bf16[16,16,128,6]{1,0,3,2:T(8,128)(2,1)S(1)} %copy.50) | data formatting | bytes 786432 | tf_op jit(solution)/shard_map/reshape | solution.py:86
  28.1 1.8 scatter_custom_fusion
  30.0 1.3 copy.52
  31.3 6.2 %all-to-all-start = ((bf16[16,2,12,768]{3,1,2,0:T(2,128)(2,1)}), bf16[16,2,12,768]{3,1,2,0:T(2,128)(2,1)S(1)}, u32[]{:S(2)}, u32[]{:S(2)}) async-start(bf16[16,2,12,768]{3,1,2,0:T(2,128)(2,1)} %copy.52), calls=%async_computation | async-start | bytes 1179648 | tf_op jit(solution)/shard_map/all_to_all | solution.py:95
  37.6 4.9 %copy.55 = bf16[8,16,2,1024]{1,0,2,3:T(8,128)(2,1)} copy(bf16[8,16,2,1024]{3,2,1,0:T(2,128)(2,1)S(1)} %copy-done.2) | data formatting | bytes 1048576 | tf_op args[2]
  42.4 6.6 %reshape.380 = bf16[2,2,65536]{2,1,0:T(2,128)(2,1)} reshape(bf16[1024,2,8,16]{3,2,1,0:T(8,128)(2,1)} %bitcast.64) | data formatting | bytes 1048576
  49.0 11.1 %reshape.375 = bf16[2,768,2048,1]{2,1,0,3:T(8,128)(2,1)} reshape(bf16[2,128,6,2,2,512]{5,4,3,2,1,0:T(2,128)(2,1)} %param.7) | data formatting | bytes 12582912 | tf_op jit(solution)/shard_map/reshape | solution.py:92
  61.0 4.4 %all-to-all-start.2 = ((bf16[2,2,65536]{2,1,0:T(2,128)(2,1)}), bf16[2,2,65536]{2,1,0:T(2,128)(2,1)}, u32[]{:S(2)}, u32[]{:S(2)}) async-start(bf16[2,2,65536]{2,1,0:T(2,128)(2,1)} %reshape.380), calls=%async_computation.2 | async-start | bytes 1048576 | tf_op jit(solution)/shard_map/all_to_all | solution.py:90
  65.4 4.4 %fusion.18 = f32[16,2,12,2048]{3,0,2,1:T(8,128)S(1)} fusion(bf16[2,768,2048,1]{2,1,0,3:T(8,128)(2,1)} %reshape.375, bf16[16,2,12,768]{3,1,2,0:T(2,128)(2,1)} %copy-done), kind=kOutput, calls=%fused_computation.28 | convolution fusion | flops 1207959552 | bytes 10027008 | tf_op jit(solution)/shard_map/sbci,bix->sbcx/dot_general | solution.py:93
  69.8 3.8 %reshape.348 = f32[16,2,12,2,2,512]{5,4,3,0,2,1:T(2,128)} reshape(f32[16,2,12,2048]{3,0,2,1:T(8,128)S(1)} %fusion.18) | data formatting | bytes 6291456 | tf_op jit(solution)/shard_map/reshape | solution.py:100
  73.5 5.4 %copy.54 = f32[16,2,12,2,2,512]{5,4,3,2,1,0:T(2,128)} copy(f32[16,2,12,2,2,512]{5,4,3,0,2,1:T(2,128)} %reshape.348) | data formatting | bytes 6291456 | tf_op jit(solution)/shard_map/reshape | solution.py:100
  79.0 6.2 %all-to-all-start.1 = ((f32[16,2,12,2,2,512]{5,4,3,2,1,0:T(2,128)}), f32[16,2,12,2,2,512]{5,4,3,2,1,0:T(2,128)S(1)}, u32[]{:S(2)}, u32[]{:S(2)}) async-start(f32[16,2,12,2,2,512]{5,4,3,2,1,0:T(2,128)} %copy.54), calls=%async_computation.1 | async-start | bytes 6291456 | tf_op jit(solution)/shard_map/all_to_all | solution.py:99
  85.2 35.0 %multiply_convert_fusion = (bf16[1024,2048]{1,0:T(8,128)(2,1)}, bf16[1024,2048]{1,0:T(8,128)(2,1)}) fusion(), kind=kLoop, calls=%fused_computation.14 | loop fusion | flops 39845888 | bytes 8388608 | tf_op jit(solution)/shard_map/convert.4
  120.2 5.2 %reshape.381 = bf16[1024,2,8,16]{3,2,1,0:T(8,128)(2,1)} reshape(bf16[2,2,65536]{2,1,0:T(2,128)(2,1)} %all-to-all-done.2) | data formatting | bytes 1048576
  125.3 5.2 %copy.56 = bf16[8,16,2,1024]{3,1,2,0:T(8,128)(2,1)} copy(bf16[8,16,2,1024]{1,0,2,3:T(8,128)(2,1)} %bitcast.63) | data formatting | bytes 1048576 | tf_op jit(solution)/shard_map/all_to_all | solution.py:90
  130.5 3.1 %reshape.353 = f32[8,16,2,2,512]{4,3,1,2,0:T(2,128)} reshape(bf16[8,16,2,1024]{3,1,2,0:T(8,128)(2,1)} %copy.56) | data formatting | bytes 1572864 | tf_op jit(solution)/shard_map/convert_element_type | solution.py:107
  133.6 1.4 copy.57
  135.1 1.0 slice_bitcast_fusion.1
  136.1 18.7 %all-to-all-done.1 = f32[16,2,12,2,2,512]{5,4,3,2,1,0:T(2,128)S(1)} async-done(((f32[16,2,12,2,2,512]{5,4,3,2,1,0:T(2,128)}), f32[16,2,12,2,2,512]{5,4,3,2,1,0:T(2,128)S(1)}, u32[]{:S(2)}, u32[]{:S(2)}) %all-to-all-start.1) | async-done | bytes 3145760 | tf_op jit(solution)/shard_map/all_to_all | solution.py:99
  154.8 4.1 %gather_fusion = f32[256,2,2,512]{3,2,1,0:T(2,128)} fusion(f32[384,2,2,512]{3,2,1,0:T(2,128)S(1)} %bitcast.65, s32[1024]{0:T(1024)S(1)} %pad_clamp_fusion), kind=kCustom, calls=%fused_computation | custom fusion | bytes 4195328 | tf_op jit(solution)/shard_map/gather | solution.py:106
  158.9 5.2 %multiply_subtract_fusion = (f32[256,2,1,512]{3,2,1,0:T(1,128)S(1)}, f32[256,2,1,512]{3,2,1,0:T(1,128)S(1)}) fusion(f32[256,2,2,512]{3,2,1,0:T(2,128)} %gather_fusion, f32[256,512]{1,0:T(8,128)} %get-tuple-element.5, f32[256,512]{1,0:T(8,128)} %get-tuple-element.4), kind=kLoop, calls=%fused_computation.32 | loop fusion | flops 1572864 | bytes 5242880 | tf_op jit(solution)/shard_map/sub | solution.py:55
  164.1 3.2 %fusion.21 = f32[16,2,2,512]{3,2,1,0:T(2,128)} fusion(f32[16,16,2,1,512]{4,3,2,1,0:T(1,128)S(1)} %bitcast.67, f32[16,16,2,1,512]{4,3,2,1,0:T(1,128)S(1)} %bitcast.66, pred[16,16]{1,0:T(8,128)(4,1)S(1)} %iota_compare_fusion.2), kind=kLoop, calls=%fused_computation.30 | loop fusion | flops 1540096 | bytes 2228480 | tf_op jit(solution)/shard_map/reduce_sum | solution.py:114
  167.4 3.6 %all-to-all-start.3 = ((f32[16,2,2,512]{3,2,1,0:T(2,128)}), f32[16,2,2,512]{3,2,1,0:T(2,128)S(1)}, u32[]{:S(2)}, u32[]{:S(2)}) async-start(f32[16,2,2,512]{3,2,1,0:T(2,128)} %fusion.21), calls=%async_computation.3 | async-start | bytes 262144 | tf_op jit(solution)/shard_map/all_to_all | solution.py:117
  171.1 4.5 %all-to-all-done.3 = f32[16,2,2,512]{3,2,1,0:T(2,128)S(1)} async-done(((f32[16,2,2,512]{3,2,1,0:T(2,128)}), f32[16,2,2,512]{3,2,1,0:T(2,128)S(1)}, u32[]{:S(2)}, u32[]{:S(2)}) %all-to-all-start.3) | async-done | bytes 131104 | tf_op jit(solution)/shard_map/all_to_all | solution.py:117
  176.0 2.7 %subtract_convert_fusion = (bf16[8,2,64,1024]{3,2,1,0:T(8,128)(2,1)S(1)}, bf16[8,2,64,1024]{3,2,1,0:T(8,128)(2,1)}) fusion(f32[8,2,1024]{2,1,0:T(2,128)S(1)} %copy.60, f32[64,1024]{1,0:T(8,128)S(1)} %get-tuple-element.11, f32[8,2,1024]{2,1,0:T(2,128)S(1)} %copy.59, f32[64,1024]{1,0:T(8,128)S(1)} %get-tuple-element.10), kind=kLoop, calls=%fused_computation.27 | loop fusion | flops 8388608 | bytes 4849664 | tf_op jit(solution)/shard_map/convert.8
  178.7 11.9 %fusion.4 = f32[1040,2048]{1,0:T(8,128)S(1)} fusion(bf16[1024,2048]{1,0:T(8,128)(2,1)S(1)} %copy-done.1, bf16[1024,2048]{1,0:T(8,128)(2,1)} %get-tuple-element.20, bf16[16,2048]{1,0:T(8,128)(2,1)S(1)} %convert_element_type.44, bf16[1024,1024]{1,0:T(8,128)(2,1)} %bitcast.71, bf16[1024,1024]{1,0:T(8,128)(2,1)S(1)} %bitcast.70), kind=kOutput, calls=%fused_computation.10 | convolution fusion | flops 8753709056 | bytes 21168128 | tf_op jit(solution)/shard_map/dot_general | solution.py:44
  (51 shorter events, 5.4 us)
Async XLA Ops:
  27.9 9.7 %copy-start.2 = (bf16[8,16,2,1024]{3,2,1,0:T(2,128)(2,1)S(1)}, bf16[8,16,2,1024]{3,2,1,0:T(2,128)(2,1)}, u32[]{:S(2)}) copy-start(bf16[8,16,2,1024]{3,2,1,0:T(2,128)(2,1)} %param.9) | copy-start | bytes 1572868
  31.3 28.8 %all-to-all-start = ((bf16[16,2,12,768]{3,1,2,0:T(2,128)(2,1)}), bf16[16,2,12,768]{3,1,2,0:T(2,128)(2,1)S(1)}, u32[]{:S(2)}, u32[]{:S(2)}) async-start(bf16[16,2,12,768]{3,1,2,0:T(2,128)(2,1)} %copy.52), calls=%async_computation | async-start | bytes 1179648 | tf_op jit(solution)/shard_map/all_to_all | solution.py:95
  60.1 0.8 copy-start
  61.0 18.0 %all-to-all-start.2 = ((bf16[2,2,65536]{2,1,0:T(2,128)(2,1)}), bf16[2,2,65536]{2,1,0:T(2,128)(2,1)}, u32[]{:S(2)}, u32[]{:S(2)}) async-start(bf16[2,2,65536]{2,1,0:T(2,128)(2,1)} %reshape.380), calls=%async_computation.2 | async-start | bytes 1048576 | tf_op jit(solution)/shard_map/all_to_all | solution.py:90
  79.0 6.2 %copy-start.3 = (f32[64]{0:T(128)S(1)}, f32[64]{0:T(128)}, u32[]{:S(2)}) copy-start(f32[64]{0:T(128)} %param.12) | copy-start | bytes 772
  79.0 6.2 %copy-start.4 = (f32[64]{0:T(128)S(1)}, f32[64]{0:T(128)}, u32[]{:S(2)}) copy-start(f32[64]{0:T(128)} %param.13) | copy-start | bytes 772
  79.0 75.8 %all-to-all-start.1 = ((f32[16,2,12,2,2,512]{5,4,3,2,1,0:T(2,128)}), f32[16,2,12,2,2,512]{5,4,3,2,1,0:T(2,128)S(1)}, u32[]{:S(2)}, u32[]{:S(2)}) async-start(f32[16,2,12,2,2,512]{5,4,3,2,1,0:T(2,128)} %copy.54), calls=%async_computation.1 | async-start | bytes 6291456 | tf_op jit(solution)/shard_map/all_to_all | solution.py:99
  167.4 8.3 %all-to-all-start.3 = ((f32[16,2,2,512]{3,2,1,0:T(2,128)}), f32[16,2,2,512]{3,2,1,0:T(2,128)S(1)}, u32[]{:S(2)}, u32[]{:S(2)}) async-start(f32[16,2,2,512]{3,2,1,0:T(2,128)} %fusion.21), calls=%async_computation.3 | async-start | bytes 262144 | tf_op jit(solution)/shard_map/all_to_all | solution.py:117
  175.8 2.9 %copy-start.1 = (bf16[1024,2048]{1,0:T(8,128)(2,1)S(1)}, bf16[1024,2048]{1,0:T(8,128)(2,1)}, u32[]{:S(2)}) copy-start(bf16[1024,2048]{1,0:T(8,128)(2,1)} %get-tuple-element.19) | copy-start | bytes 12582916
where the time goes:
time: 194 us; the launch traced here: 193 us
  local copies, waits for them, and re-layouts  68.2 us (35%)
  other arithmetic  47.8 us (25%)
  waiting for transfers between devices  23.2 us (12%)
  starting transfers between devices  20.4 us (11%)
  matrix products  16.3 us (8%)
  blocking collectives  15.3 us (8%)
    another operation x4, other arithmetic  38.3 us
    unnamed x16, local copies, waits for them, and re-layouts  19.6 us
    all_to_all x1, waiting for transfers between devices, body(): lax.all_to_all(product.reshape(product.shape[:3] + (comp_count, 2, freq_l...  18.7 us
    dot_general x1, matrix products, oscillate(): outcome = jnp.dot(stacked, dft_table, preferred_element_type=jnp.float32)  11.9 us
    reshape x1, local copies, waits for them, and re-layouts, body(): green.reshape(blocks_local, inner_width, comp_count * 2 * freq_local)  11.1 us
    reshape x2, local copies, waits for them, and re-layouts, body(): product.reshape(product.shape[:3] + (comp_count, 2, freq_local))  9.22 us
    all_gather x1, blocking collectives, body(): lax.all_gather(slip_weights, 'rup', axis=0, tiled=True)  6.55 us
    all_to_all x1, starting transfers between devices, body(): lax.all_to_all(weight_send, 'fault', split_axis=0, concat_axis=0, tiled=T...  6.24 us
  transfers between devices with their start and end apart: 4, of which 2 were waited for; matrix products, arithmetic and copies ran while one was open for 45% of the time, Pallas kernels for 0%

commit v1 on v0

v1 whole, which is shorter than its diff:
```python
import math

import jax
import jax.numpy as jnp
from jax import lax
from jax.sharding import PartitionSpec as P


def inverse_table(freq_count):
    sample_count = 2 * freq_count
    freq_index = jnp.arange(freq_count, dtype=jnp.int32)
    time_index = jnp.arange(sample_count, dtype=jnp.int32)
    phase_index = freq_index[:, None] * time_index[None, :] % sample_count
    phase_angle = phase_index.astype(jnp.float32) * jnp.float32(2.0 * math.pi / sample_count)
    norm_scale = jnp.float32(1.0 / math.sqrt(freq_count))
    cosines = jnp.cos(phase_angle) * norm_scale
    sines = -jnp.sin(phase_angle) * norm_scale
    return jnp.concatenate([cosines, sines], axis=0).astype(jnp.bfloat16)


def oscillator_gain(natural_freq, damping, freq_count):
    omega_f = jnp.arange(freq_count, dtype=jnp.float32) * jnp.float32(math.pi / freq_count)
    omega_nat = jnp.float32(math.pi) * natural_freq[:, None]
    stiffness = omega_nat * omega_nat
    den_real = stiffness - omega_f[None, :] * omega_f[None, :]
    den_imag = 2.0 * damping[:, None] * omega_nat * omega_f[None, :]
    magnitude = den_real * den_real + den_imag * den_imag
    return (stiffness * den_real / magnitude, -stiffness * den_imag / magnitude)


def oscillate(spectra, gain_real, gain_imag, dft_table):
    rupture_count = spectra.shape[0]
    comp_count = spectra.shape[1]
    freq_count = spectra.shape[3]
    period_count = gain_real.shape[0]
    spec_real = spectra[:, :, 0][:, :, None, :]
    spec_imag = spectra[:, :, 1][:, :, None, :]
    resp_real = gain_real * spec_real - gain_imag * spec_imag
    resp_imag = gain_real * spec_imag + gain_imag * spec_real
    resp_rows = jnp.concatenate([resp_real, resp_imag], axis=3).astype(jnp.bfloat16)
    resp_rows = resp_rows.reshape(rupture_count * comp_count * period_count, 2 * freq_count)
    wave_rows = spectra.reshape(rupture_count * comp_count, 2 * freq_count).astype(jnp.bfloat16)
    stacked = jnp.concatenate([resp_rows, wave_rows], axis=0)
    outcome = jnp.dot(stacked, dft_table, preferred_element_type=jnp.float32)
    split_at = rupture_count * comp_count * period_count
    peaks = jnp.max(jnp.abs(outcome[:split_at]), axis=1).reshape(
        rupture_count, comp_count, period_count
    )
    waveform = outcome[split_at:].reshape(rupture_count, comp_count, 2 * freq_count)
    return (waveform, peaks)


def body(green, slip_weights, slip_spectra, block_lists, block_counts, natural_freq, damping):
    fault_count = lax.axis_size("fault")
    group_size = lax.axis_size("rup")
    owned_count, slot_width = block_lists.shape
    blocks_local, points, terms, comp_count, _, freq_local = green.shape
    freq_count = slip_spectra.shape[3]
    inner_width = points * terms
    block_total = blocks_local * fault_count
    device_count = fault_count * group_size
    slot_rows = owned_count * slot_width
    axes = ("fault", "rup")
    slot_index = lax.broadcasted_iota(jnp.int32, (owned_count, slot_width), 1)
    named = jnp.where(slot_index < block_counts[:, None], block_lists, -1).reshape(1, slot_rows)
    pick_shape = (block_total, owned_count, slot_rows)
    row_block = lax.broadcasted_iota(jnp.int32, pick_shape, 0)
    row_owner = lax.broadcasted_iota(jnp.int32, pick_shape, 1)
    col_owner = lax.broadcasted_iota(jnp.int32, pick_shape, 2) // slot_width
    pick = ((named[None] == row_block) & (row_owner == col_owner)).astype(jnp.bfloat16)
    pick = pick.reshape(block_total * owned_count, slot_rows)
    weight_rows = slip_weights.transpose(0, 1, 3, 2).reshape(slot_rows, inner_width)
    weight_send = jnp.dot(pick, weight_rows, preferred_element_type=jnp.float32).astype(jnp.bfloat16)
    weight_send = jnp.broadcast_to(
        weight_send.reshape(fault_count, 1, blocks_local, owned_count, inner_width),
        (fault_count, group_size, blocks_local, owned_count, inner_width),
    ).reshape(device_count, blocks_local, owned_count, inner_width)
    weight_recv = lax.all_to_all(weight_send, axes, split_axis=0, concat_axis=0, tiled=True)
    slip_rows = slip_spectra.reshape(slot_rows, 2, group_size, freq_local).transpose(0, 2, 1, 3)
    slip_rows = slip_rows.reshape(slot_rows, 2 * freq_count)
    slip_send = jnp.dot(pick, slip_rows, preferred_element_type=jnp.float32).astype(jnp.bfloat16)
    slip_send = slip_send.reshape(
        fault_count, blocks_local, owned_count, group_size, 2, freq_local
    ).transpose(0, 3, 1, 4, 2, 5)
    slip_send = slip_send.reshape(device_count, blocks_local, 2, owned_count, freq_local)
    slip_recv = lax.all_to_all(slip_send, axes, split_axis=0, concat_axis=0, tiled=True)
    tile_mats = green.transpose(0, 2, 1, 3, 4, 5).reshape(
        blocks_local, inner_width, comp_count * 2 * freq_local
    )
    total_real, total_imag = 0.0, 0.0
    for b in range(blocks_local):
        rows = weight_recv[:, b].reshape(device_count * owned_count, inner_width)
        product = jnp.dot(rows, tile_mats[b], preferred_element_type=jnp.float32)
        product = product.reshape(device_count, owned_count, comp_count, 2, freq_local)
        slip_f = slip_recv[:, b].astype(jnp.float32)
        slip_real = slip_f[:, 0][:, :, None]
        slip_imag = slip_f[:, 1][:, :, None]
        prod_real, prod_imag = product[:, :, :, 0], product[:, :, :, 1]
        total_real = total_real + prod_real * slip_real - prod_imag * slip_imag
        total_imag = total_imag + prod_real * slip_imag + prod_imag * slip_real
    partial = jnp.stack([total_real, total_imag], axis=1).astype(jnp.bfloat16)
    partial = partial.transpose(0, 3, 1, 2, 4)
    returned = lax.all_to_all(partial, axes, split_axis=0, concat_axis=0, tiled=True)
    returned = returned.reshape(
        fault_count, group_size, comp_count, 2, owned_count, freq_local
    ).astype(jnp.float32)
    spectra = jnp.sum(returned, axis=0).transpose(3, 1, 2, 0, 4)
    spectra = spectra.reshape(owned_count, comp_count, 2, freq_count)
    gain_real, gain_imag = oscillator_gain(natural_freq, damping, freq_count)
    dft_table = inverse_table(freq_count)
    waveform, peaks = oscillate(spectra, gain_real, gain_imag, dft_table)
    return (waveform, peaks)


def solution(mesh):
    return jax.shard_map(
        body,
        mesh=mesh,
        in_specs=(
            P("fault", None, None, None, None, "rup"),
            P(("fault", "rup"), None, None, None),
            P(("fault", "rup"), None, None, None),
            P(("fault", "rup"), None),
            P(("fault", "rup")),
            P(),
            P(),
        ),
        out_specs=(P(("fault", "rup"), None, None), P(("fault", "rup"), None, None)),
        check_vma=False,
    )
```

time: 194 us -> 137 us (0.71)
  the two profiles are of different devices: /device:TPU:10 before, /device:TPU:0 now
where the time goes in v1:
time: 137 us
  other arithmetic  42.4 us (31%)
  local copies, waits for them, and re-layouts  39.8 us (29%)
  matrix products  18.5 us (14%)
  waiting for transfers between devices  18.1 us (13%)
  starting transfers between devices  17 us (12%)
    another operation x3, other arithmetic  38.8 us
    all_to_all x1, waiting for transfers between devices, body(): lax.all_to_all(weight_send, axes, split_axis=0, concat_axis=0, tiled=True)  18.1 us
    slice x3, local copies, waits for them, and re-layouts, body(): product = jnp.dot(rows, tile_mats[b], preferred_element_type=jnp.float32)  14.1 us
    dot_general x1, matrix products, oscillate(): outcome = jnp.dot(stacked, dft_table, preferred_element_type=jnp.float32)  11.9 us
    dot_general x2, local copies, waits for them, and re-layouts, body(): product = jnp.dot(rows, tile_mats[b], preferred_element_type=jnp.float32)  9.46 us
    squeeze x2, local copies, waits for them, and re-layouts, body(): product = jnp.dot(rows, tile_mats[b], preferred_element_type=jnp.float32)  8.08 us
    all_to_all x1, starting transfers between devices, body(): lax.all_to_all(weight_send, axes, split_axis=0, concat_axis=0, tiled=True)  7.32 us
    all_to_all x1, starting transfers between devices, body(): lax.all_to_all(partial, axes, split_axis=0, concat_axis=0, tiled=True)  5.95 us
  transfers between devices with their start and end apart: 3, of which 1 were waited for; matrix products, arithmetic and copies ran while one was open for 55% of the time, Pallas kernels for 0%

profile of v1, /device:TPU:0, one launch (start us, length us, event | category | flops | bytes accessed | tf_op | source)
XLA Modules:
  0.0 136.7 jit_solution(2393912495998433137)
XLA Ops:
  0.7 0.8 fusion.42
  1.8 1.0 copy.54
  2.8 0.3 convolution_convert_fusion.1
  3.1 1.0 broadcast_in_dim.10
  4.0 7.3 %all-to-all-start = ((bf16[32,2,8,768]{3,2,1,0:T(8,128)(2,1)}), bf16[32,2,8,768]{3,2,1,0:T(8,128)(2,1)S(1)}, u32[]{:S(2)}, u32[]{:S(2)}) async-start(bf16[32,2,8,768]{3,2,1,0:T(8,128)(2,1)} %bitcast.2), calls=%async_computation | async-start | bytes 1572864 | tf_op jit(solution)/shard_map/all_to_all | solution.py:78
  11.4 0.3 reshape.334
  11.7 0.5 copy.60
  12.3 0.5 convolution_convert_fusion
  12.8 1.1 copy.61
  13.8 18.1 %all-to-all-done = bf16[32,2,8,768]{3,2,1,0:T(8,128)(2,1)S(1)} async-done(((bf16[32,2,8,768]{3,2,1,0:T(8,128)(2,1)}), bf16[32,2,8,768]{3,2,1,0:T(8,128)(2,1)S(1)}, u32[]{:S(2)}, u32[]{:S(2)}) %all-to-all-start) | async-done | bytes 786464 | tf_op jit(solution)/shard_map/all_to_all | solution.py:78
  32.0 3.7 %all-to-all-start.1 = ((bf16[32,2,2,8,512]{4,3,2,1,0:T(8,128)(2,1)}), bf16[32,2,2,8,512]{4,3,2,1,0:T(8,128)(2,1)}, u32[]{:S(2)}, u32[]{:S(2)}) async-start(bf16[32,2,2,8,512]{4,3,2,1,0:T(8,128)(2,1)} %bitcast.16), calls=%async_computation.1 | async-start | bytes 2097152 | tf_op jit(solution)/shard_map/all_to_all | solution.py:86
  35.7 7.9 %fusion.46 = (bf16[1,6,128,2,2,512]{5,4,3,1,2,0:T(2,128)(2,1)S(1)}, bf16[1,6,128,2,2,512]{5,4,3,1,2,0:T(2,128)(2,1)}) fusion(bf16[2,6,128,2,2,512]{5,4,3,1,2,0:T(2,128)(2,1)} %bitcast.108), kind=kLoop, calls=%fused_computation.87 | loop fusion | bytes 12582912 | tf_op jit(solution)/shard_map/slice | solution.py:93
  43.6 2.2 %copy.63 = bf16[1,6,128,2,2,512]{5,4,3,2,1,0:T(2,128)(2,1)S(1)} copy(bf16[1,6,128,2,2,512]{5,4,3,1,2,0:T(2,128)(2,1)S(1)} %get-tuple-element.4) | data formatting | bytes 6291456 | tf_op jit(solution)/shard_map/slice | solution.py:93
  45.8 4.0 %squeeze.23 = bf16[768,2048]{1,0:T(8,128)(2,1)} reshape(bf16[1,6,128,2,2,512]{5,4,3,2,1,0:T(2,128)(2,1)S(1)} %copy.63) | data formatting | bytes 6291456 | tf_op jit(solution)/shard_map/squeeze | solution.py:93
  49.9 4.7 %copy.64 = bf16[2048,768]{1,0:T(8,128)(2,1)} copy(bf16[2048,768]{0,1:T(8,128)(2,1)} %bitcast.106) | data formatting | bytes 6291456 | tf_op jit(solution)/shard_map/dot_general | solution.py:93
  54.5 4.0 %copy.56 = bf16[1,6,128,2,2,512]{5,4,3,2,1,0:T(2,128)(2,1)S(1)} copy(bf16[1,6,128,2,2,512]{5,4,3,1,2,0:T(2,128)(2,1)} %get-tuple-element.5) | data formatting | bytes 6291456 | tf_op jit(solution)/shard_map/slice | solution.py:93
  58.6 4.0 %squeeze.20 = bf16[768,2048]{1,0:T(8,128)(2,1)} reshape(bf16[1,6,128,2,2,512]{5,4,3,2,1,0:T(2,128)(2,1)S(1)} %copy.56) | data formatting | bytes 6291456 | tf_op jit(solution)/shard_map/squeeze | solution.py:93
  62.6 4.8 %copy.57 = bf16[2048,768]{1,0:T(8,128)(2,1)} copy(bf16[2048,768]{0,1:T(8,128)(2,1)} %bitcast.107) | data formatting | bytes 6291456 | tf_op jit(solution)/shard_map/dot_general | solution.py:93
  67.4 3.5 %fusion.16 = f32[32,8,2,2,512]{4,1,2,0,3:T(8,128)} fusion(bf16[2,2,512,768,1]{3,2,1,0,4:T(8,128)(2,1)S(1)} %bitcast.111, bf16[32,2,8,768]{3,2,1,0:T(8,128)(2,1)} %copy-done.5), kind=kOutput, calls=%fused_computation.24 | convolution fusion | flops 805306368 | bytes 5636096 | tf_op jit(solution)/shard_map/dot_general | solution.py:93
  70.9 2.3 %fusion.20 = f32[32,8,2,2,512]{4,1,3,2,0:T(8,128)} fusion(bf16[2,2,512,768,1]{3,2,1,0,4:T(8,128)(2,1)S(1)} %bitcast.112, bf16[32,2,8,768]{3,2,1,0:T(8,128)(2,1)S(1)} %copy-done.6), kind=kOutput, calls=%fused_computation.46 | convolution fusion | flops 805306368 | bytes 5636096 | tf_op jit(solution)/shard_map/dot_general | solution.py:93
  73.3 1.6 %fusion.19 = (f32[32,2,8,512]{3,2,1,0:T(8,128)S(1)}, f32[32,2,8,512]{3,2,1,0:T(8,128)S(1)}) fusion(bf16[32,2,2,8,512]{4,3,2,1,0:T(8,128)(2,1)} %all-to-all-done.1), kind=kLoop, calls=%fused_computation.43 | loop fusion | flops 524288 | bytes 3145728 | tf_op jit(solution)/shard_map/convert_element_type | solution.py:95
  75.2 0.6 copy-done.4
  75.8 1.1 subtract_convert_fusion.1
  77.0 1.2 copy.67
  78.2 6.0 %all-to-all-start.2 = ((bf16[32,2,2,8,512]{4,3,1,2,0:T(8,128)(2,1)}), bf16[32,2,2,8,512]{4,3,1,2,0:T(8,128)(2,1)S(1)}, u32[]{:S(2)}, u32[]{:S(2)}) async-start(bf16[32,2,2,8,512]{4,3,1,2,0:T(8,128)(2,1)} %copy.67), calls=%async_computation.2 | async-start | bytes 2097152 | tf_op jit(solution)/shard_map/all_to_all | solution.py:103
  84.4 35.0 %multiply_convert_fusion = (bf16[1024,2048]{1,0:T(8,128)(2,1)}, bf16[1024,2048]{1,0:T(8,128)(2,1)}) fusion(), kind=kLoop, calls=%fused_computation.12 | loop fusion | flops 39845888 | bytes 8388608 | tf_op jit(solution)/shard_map/convert.4
  119.3 0.2 convert_reduce_fusion
  120.1 2.7 %subtract_convert_fusion = (bf16[8,2,64,1024]{3,2,1,0:T(8,128)(2,1)S(1)}, bf16[8,2,64,1024]{3,2,1,0:T(8,128)(2,1)}) fusion(f32[8,2,1024]{2,1,0:T(2,128)S(1)} %copy.71, f32[64,1024]{1,0:T(8,128)S(1)} %get-tuple-element.17, f32[8,2,1024]{2,1,0:T(2,128)S(1)} %copy.70, f32[64,1024]{1,0:T(8,128)S(1)} %get-tuple-element.16), kind=kLoop, calls=%fused_computation.23 | loop fusion | flops 8388608 | bytes 4849664 | tf_op jit(solution)/shard_map/convert.8
  122.8 11.9 %fusion.4 = f32[1040,2048]{1,0:T(8,128)S(1)} fusion(bf16[1024,2048]{1,0:T(8,128)(2,1)S(1)} %copy-done, bf16[1024,2048]{1,0:T(8,128)(2,1)} %get-tuple-element.26, bf16[16,2048]{1,0:T(8,128)(2,1)S(1)} %convert_element_type.49, bf16[1024,1024]{1,0:T(8,128)(2,1)} %bitcast.114, bf16[1024,1024]{1,0:T(8,128)(2,1)S(1)} %bitcast.113), kind=kOutput, calls=%fused_computation.8 | convolution fusion | flops 8753709056 | bytes 21168128 | tf_op jit(solution)/shard_map/dot_general | solution.py:44
  134.7 0.6 fusion.3
  135.3 0.7 reshape.325
  136.1 0.7 reshape.326
  (43 shorter events, 1.3 us)
Async XLA Ops:
  0.6 10.7 %copy-start.7 = (bf16[8,16,2,1024]{3,2,1,0:T(2,128)(2,1)S(1)}, bf16[8,16,2,1024]{3,2,1,0:T(2,128)(2,1)}, u32[]{:S(2)}) copy-start(bf16[8,16,2,1024]{3,2,1,0:T(2,128)(2,1)} %param.9) | copy-start | bytes 1572868
  4.0 27.9 %all-to-all-start = ((bf16[32,2,8,768]{3,2,1,0:T(8,128)(2,1)}), bf16[32,2,8,768]{3,2,1,0:T(8,128)(2,1)S(1)}, u32[]{:S(2)}, u32[]{:S(2)}) async-start(bf16[32,2,8,768]{3,2,1,0:T(8,128)(2,1)} %bitcast.2), calls=%async_computation | async-start | bytes 1572864 | tf_op jit(solution)/shard_map/all_to_all | solution.py:78
  32.0 11.7 %copy-start.5 = (bf16[32,2,8,768]{3,2,1,0:T(8,128)(2,1)}, bf16[32,2,8,768]{3,2,1,0:T(8,128)(2,1)S(1)}, u32[]{:S(2)}) copy-start(bf16[32,2,8,768]{3,2,1,0:T(8,128)(2,1)S(1)} %all-to-all-done) | copy-start | bytes 2359300
  32.0 41.3 %all-to-all-start.1 = ((bf16[32,2,2,8,512]{4,3,2,1,0:T(8,128)(2,1)}), bf16[32,2,2,8,512]{4,3,2,1,0:T(8,128)(2,1)}, u32[]{:S(2)}, u32[]{:S(2)}) async-start(bf16[32,2,2,8,512]{4,3,2,1,0:T(8,128)(2,1)} %bitcast.16), calls=%async_computation.1 | async-start | bytes 2097152 | tf_op jit(solution)/shard_map/all_to_all | solution.py:86
  62.6 4.8 %copy-start.1 = (bf16[2048,768]{1,0:T(8,128)(2,1)S(1)}, bf16[2048,768]{1,0:T(8,128)(2,1)}, u32[]{:S(2)}) copy-start(bf16[2048,768]{1,0:T(8,128)(2,1)} %copy.64) | copy-start | bytes 9437188
  67.4 3.5 %copy-start.2 = (bf16[2048,768]{1,0:T(8,128)(2,1)S(1)}, bf16[2048,768]{1,0:T(8,128)(2,1)}, u32[]{:S(2)}) copy-start(bf16[2048,768]{1,0:T(8,128)(2,1)} %copy.57) | copy-start | bytes 9437188
  67.4 3.5 %copy-start.6 = (bf16[32,2,8,768]{3,2,1,0:T(8,128)(2,1)S(1)}, bf16[32,2,8,768]{3,2,1,0:T(8,128)(2,1)}, u32[]{:S(2)}) copy-start(bf16[32,2,8,768]{3,2,1,0:T(8,128)(2,1)} %copy-done.5) | copy-start | bytes 2359300
  73.2 1.9 %copy-start.3 = (f32[32,8,2,2,512]{4,1,2,0,3:T(8,128)S(1)}, f32[32,8,2,2,512]{4,1,2,0,3:T(8,128)}, u32[]{:S(2)}) copy-start(f32[32,8,2,2,512]{4,1,2,0,3:T(8,128)} %fusion.16) | copy-start | bytes 6291460
  73.3 2.5 %copy-start.4 = (f32[32,8,2,2,512]{4,1,3,2,0:T(8,128)S(1)}, f32[32,8,2,2,512]{4,1,3,2,0:T(8,128)}, u32[]{:S(2)}) copy-start(f32[32,8,2,2,512]{4,1,3,2,0:T(8,128)} %fusion.20) | copy-start | bytes 6291460
  76.9 7.3 %copy-start.8 = (f32[64]{0:T(128)S(1)}, f32[64]{0:T(128)}, u32[]{:S(2)}) copy-start(f32[64]{0:T(128)} %param.12) | copy-start | bytes 772
  76.9 7.3 %copy-start.9 = (f32[64]{0:T(128)S(1)}, f32[64]{0:T(128)}, u32[]{:S(2)}) copy-start(f32[64]{0:T(128)} %param.13) | copy-start | bytes 772
  78.2 41.2 %all-to-all-start.2 = ((bf16[32,2,2,8,512]{4,3,1,2,0:T(8,128)(2,1)}), bf16[32,2,2,8,512]{4,3,1,2,0:T(8,128)(2,1)S(1)}, u32[]{:S(2)}, u32[]{:S(2)}) async-start(bf16[32,2,2,8,512]{4,3,1,2,0:T(8,128)(2,1)} %copy.67), calls=%async_computation.2 | async-start | bytes 2097152 | tf_op jit(solution)/shard_map/all_to_all | solution.py:103
  119.9 2.9 %copy-start = (bf16[1024,2048]{1,0:T(8,128)(2,1)S(1)}, bf16[1024,2048]{1,0:T(8,128)(2,1)}, u32[]{:S(2)}) copy-start(bf16[1024,2048]{1,0:T(8,128)(2,1)} %get-tuple-element.25) | copy-start | bytes 12582916

commit v2 on v1

v2 whole, which is shorter than its diff:
```python
import math

import jax
import jax.numpy as jnp
from jax import lax
from jax.experimental import pallas as pl
from jax.experimental.pallas import tpu as pltpu
from jax.sharding import PartitionSpec as P

LANES = 128


def phase_waves(freq_index, time_index, sample_count):
    phase = freq_index[:, None] * time_index[None, :] % sample_count
    angle = phase.astype(jnp.float32) * jnp.float32(2.0 * math.pi / sample_count)
    return jnp.cos(angle), jnp.sin(angle)


def half_tables(freq_count):
    sample_count = 2 * freq_count
    scale = jnp.float32(1.0 / math.sqrt(freq_count))
    fine = jnp.arange(LANES, dtype=jnp.int32)
    coarse = jnp.arange(freq_count // LANES, dtype=jnp.int32) * LANES
    cosines, sines = [], []
    for parity in range(2):
        freq_index = 2 * jnp.arange(freq_count // 2, dtype=jnp.int32) + parity
        cos_f, sin_f = phase_waves(freq_index, fine, sample_count)
        cos_c, sin_c = phase_waves(freq_index, coarse, sample_count)
        cos_f, sin_f, cos_c, sin_c = lax.optimization_barrier(
            (cos_f * scale, sin_f * scale, cos_c, sin_c)
        )
        cos_parts, sin_parts = [], []
        for a in range(freq_count // LANES):
            ca, sa = cos_c[:, a : a + 1], sin_c[:, a : a + 1]
            cos_parts.append((ca * cos_f - sa * sin_f).astype(jnp.bfloat16))
            sin_parts.append((-(sa * cos_f + ca * sin_f)).astype(jnp.bfloat16))
        cosines.append(jnp.concatenate(cos_parts, axis=1))
        sines.append(jnp.concatenate(sin_parts, axis=1))
    return (cosines[0], cosines[1], sines[0], sines[1])


def split_gain(natural_freq, damping, freq_count):
    freq_index = jnp.arange(freq_count, dtype=jnp.float32).reshape(freq_count // 2, 2).T
    freq_index = freq_index.reshape(1, 2, 1, freq_count // 2)
    omega_f = freq_index * jnp.float32(math.pi / freq_count)
    omega_nat = (jnp.float32(math.pi) * natural_freq)[None, None, :, None]
    stiffness = omega_nat * omega_nat
    den_real = stiffness - omega_f * omega_f
    den_imag = 2.0 * damping[None, None, :, None] * omega_nat * omega_f
    magnitude = den_real * den_real + den_imag * den_imag
    return jnp.concatenate(
        [stiffness * den_real / magnitude, -stiffness * den_imag / magnitude], axis=0
    )


def oscillate_kernel(spec_ref, gain_ref, ce_ref, co_ref, se_ref, so_ref, wave_ref, peak_ref):
    step = pl.program_id(0)
    rows_per = peak_ref.shape[1]
    period_count, half = gain_ref.shape[2], gain_ref.shape[3]
    f32 = jnp.float32
    tables = (ce_ref, co_ref, se_ref, so_ref)

    @pl.when(step == 0)
    def _():
        parts = [
            jnp.dot(spec_ref[i // 2, i % 2].astype(jnp.bfloat16), tables[i][...], preferred_element_type=f32)
            for i in range(4)
        ]
        even, odd = parts[0] + parts[2], parts[1] + parts[3]
        wave_ref[:, : 2 * half] = even + odd
        wave_ref[:, 2 * half :] = even - odd

    stacked = [[], [], [], []]
    for r in range(rows_per):
        row = pl.ds(step * rows_per + r, 1)
        for parity in range(2):
            sr, si = spec_ref[0, parity, row, :], spec_ref[1, parity, row, :]
            gr, gi = gain_ref[0, parity], gain_ref[1, parity]
            stacked[parity].append((gr * sr - gi * si).astype(jnp.bfloat16))
            stacked[2 + parity].append((gr * si + gi * sr).astype(jnp.bfloat16))
    rows = [jnp.concatenate(group, axis=0) for group in stacked]
    ce, co, se, so = (
        jnp.dot(rows[i], tables[i][:, :half], preferred_element_type=f32) for i in range(4)
    )
    best = jnp.maximum(
        jnp.abs(ce + co) + jnp.abs(se + so), jnp.abs(ce - co) + jnp.abs(se - so)
    )
    best = jnp.max(best, axis=1, keepdims=True)
    lane = lax.broadcasted_iota(jnp.int32, (1, half), 1)
    signs = jnp.where(lane % 2 == 0, f32(1.0), f32(-1.0)) * f32(1.0 / math.sqrt(2 * half))
    middle = jnp.abs(jnp.sum(rows[0].astype(f32) * signs, axis=1, keepdims=True)) + jnp.abs(
        jnp.sum(rows[3].astype(f32) * signs, axis=1, keepdims=True)
    )
    best = jnp.maximum(best, middle)
    shape = (period_count, period_count)
    diag = lax.broadcasted_iota(jnp.int32, shape, 0) == lax.broadcasted_iota(jnp.int32, shape, 1)
    for r in range(rows_per):
        column = best[r * period_count : (r + 1) * period_count]
        peak_ref[0, r : r + 1, :] = jnp.sum(
            jnp.where(diag, column, f32(0.0)), axis=0, keepdims=True
        )


def oscillate(spectra, gain, tables):
    row_count, half = spectra.shape[2:]
    period_count = gain.shape[2]
    rows_per = math.gcd(row_count, 4)
    steps = row_count // rows_per
    whole = lambda shape: pl.BlockSpec(shape, lambda i: (0,) * len(shape), pipeline_mode=pl.Buffered(1))
    wave, peak = pl.pallas_call(
        oscillate_kernel,
        grid=(steps,),
        in_specs=[whole(spectra.shape), whole(gain.shape)] + [whole(t.shape) for t in tables],
        out_specs=[
            pl.BlockSpec((row_count, 4 * half), lambda i: (0, 0)),
            pl.BlockSpec((1, rows_per, period_count), lambda i: (i, 0, 0)),
        ],
        out_shape=[
            jax.ShapeDtypeStruct((row_count, 4 * half), jnp.float32),
            jax.ShapeDtypeStruct((steps, rows_per, period_count), jnp.float32),
        ],
        compiler_params=pltpu.CompilerParams(vmem_limit_bytes=40 << 20),
    )(spectra, gain, *tables)
    return wave, peak


def body(green, slip_weights, slip_spectra, block_lists, block_counts, natural_freq, damping):
    fault_count = lax.axis_size("fault")
    group_size = lax.axis_size("rup")
    owned_count, slot_width = block_lists.shape
    blocks_local, points, terms, comp_count, _, freq_local = green.shape
    freq_count = slip_spectra.shape[3]
    inner_width = points * terms
    block_total = blocks_local * fault_count
    device_count = fault_count * group_size
    slot_rows = owned_count * slot_width
    axes = ("fault", "rup")
    bf16, f32 = jnp.bfloat16, jnp.float32
    slot_index = lax.broadcasted_iota(jnp.int32, (owned_count, slot_width), 1)
    named = jnp.where(slot_index < block_counts[:, None], block_lists, -1).reshape(1, slot_rows)
    pick_shape = (block_total, owned_count, slot_rows)
    row_block = lax.broadcasted_iota(jnp.int32, pick_shape, 0)
    row_owner = lax.broadcasted_iota(jnp.int32, pick_shape, 1)
    col_owner = lax.broadcasted_iota(jnp.int32, pick_shape, 2) // slot_width
    pick = ((named[None] == row_block) & (row_owner == col_owner)).astype(bf16)
    pick = pick.reshape(block_total * owned_count, slot_rows)
    from_index = jnp.arange(inner_width, dtype=jnp.int32)
    to_index = (from_index % points) * terms + from_index // points
    turn = (to_index[:, None] == from_index[None, :]).astype(bf16)
    weight_rows = slip_weights.transpose(0, 1, 3, 2).reshape(slot_rows, inner_width)
    weight_rows = jnp.dot(weight_rows, turn, preferred_element_type=f32).astype(bf16)
    weight_send = jnp.dot(pick, weight_rows, preferred_element_type=f32).astype(bf16)
    weight_send = jnp.broadcast_to(
        weight_send.reshape(fault_count, 1, blocks_local, owned_count, inner_width),
        (fault_count, group_size, blocks_local, owned_count, inner_width),
    ).reshape(device_count, blocks_local, owned_count, inner_width)
    weight_recv = lax.all_to_all(weight_send, axes, split_axis=0, concat_axis=0, tiled=True)
    slip_rows = slip_spectra.reshape(slot_rows, 2, group_size, freq_local).transpose(0, 2, 1, 3)
    slip_rows = slip_rows.reshape(slot_rows, 2 * freq_count)
    slip_send = jnp.dot(pick, slip_rows, preferred_element_type=f32).astype(bf16)
    slip_send = slip_send.reshape(
        fault_count, blocks_local, owned_count, group_size, 2, freq_local
    ).transpose(0, 3, 1, 4, 2, 5)
    slip_send = slip_send.reshape(device_count, blocks_local, 2, owned_count, freq_local)
    slip_recv = lax.all_to_all(slip_send, axes, split_axis=0, concat_axis=0, tiled=True)
    tile_mats = green.reshape(blocks_local, inner_width, comp_count * 2 * freq_local)
    product = jnp.einsum("sbqi,bix->sbqx", weight_recv, tile_mats, preferred_element_type=f32)
    slip_f = slip_recv.astype(f32)
    ones = []
    for c in range(comp_count):
        at = 2 * c * freq_local
        prod_real = product[:, :, :, at : at + freq_local]
        prod_imag = product[:, :, :, at + freq_local : at + 2 * freq_local]
        slip_real, slip_imag = slip_f[:, :, 0], slip_f[:, :, 1]
        ones.append(jnp.sum(prod_real * slip_real - prod_imag * slip_imag, axis=1))
        ones.append(jnp.sum(prod_real * slip_imag + prod_imag * slip_real, axis=1))
    partial = jnp.stack([one.astype(bf16) for one in ones], axis=1)
    order = jnp.arange(freq_local, dtype=jnp.int32)
    split_to = (order % 2) * (freq_local // 2) + order // 2
    deal = (split_to[:, None] == order[None, :]).astype(bf16)
    partial = jnp.dot(
        partial.reshape(device_count * comp_count * 2 * owned_count, freq_local),
        deal,
        preferred_element_type=f32,
    ).astype(bf16)
    partial = partial.reshape(device_count, comp_count * 2, owned_count, freq_local)
    returned = lax.all_to_all(partial, axes, split_axis=0, concat_axis=0, tiled=True)
    returned = returned.reshape(
        fault_count, group_size, comp_count, 2, owned_count, 2, freq_local // 2
    ).astype(f32)
    spectra = jnp.sum(returned, axis=0).transpose(2, 4, 1, 3, 0, 5)
    spectra = spectra.reshape(2, 2, comp_count * owned_count, freq_count // 2)
    gain = split_gain(natural_freq, damping, freq_count)
    tables = half_tables(freq_count)
    wave, peak = oscillate(spectra, gain, tables)
    period_count = natural_freq.shape[0]
    waveform = wave.reshape(comp_count, owned_count, 2 * freq_count).transpose(1, 0, 2)
    peaks = peak.reshape(comp_count, owned_count, period_count).transpose(1, 0, 2)
    return (waveform, peaks)


def solution(mesh):
    return jax.shard_map(
        body,
        mesh=mesh,
        in_specs=(
            P("fault", None, None, None, None, "rup"),
            P(("fault", "rup"), None, None, None),
            P(("fault", "rup"), None, None, None),
            P(("fault", "rup"), None),
            P(("fault", "rup")),
            P(),
            P(),
        ),
        out_specs=(P(("fault", "rup"), None, None), P(("fault", "rup"), None, None)),
        check_vma=False,
    )
```

time: 137 us -> 110 us (0.80)
  other arithmetic: 42.4 us -> 15.1 us
  waiting for transfers between devices: 18.1 us -> 41.5 us
  local copies, waits for them, and re-layouts: 39.8 us -> 21.2 us
  matrix products: 18.5 us -> 10.1 us
  Pallas kernels: 0 us -> 4.82 us
  starting transfers between devices: 17 us -> 15.1 us
    another operation x3 -> x1, other arithmetic: 38.8 us -> 0.13 us  [body(): partial = jnp.stack([one.astype(bf16) for one in ones], axis=1)]
    all_to_all x1, waiting for transfers between devices: 0.01 us -> 20.9 us  [body(): lax.all_to_all(partial, axes, split_axis=0, concat_axis=0, tiled=True)]
    all_to_all x1, waiting for transfers between devices: 0.01 us -> 17.9 us  [body(): lax.all_to_all(slip_send, axes, split_axis=0, concat_axis=0, tiled=True)]
    all_to_all x1, waiting for transfers between devices: 18.1 us -> 2.63 us  [body(): lax.all_to_all(weight_send, axes, split_axis=0, concat_axis=0, tiled=True)]
    slice x4, local copies, waits for them, and re-layouts: 14.1 us -> 0.06 us  [half_tables(): ca, sa = (cos_c[:, a:a + 1], sin_c[:, a:a + 1])]
    reshape x3, local copies, waits for them, and re-layouts: 1.52 us -> 12.6 us  [the longest x1 11.2 us: body(): green.reshape(blocks_local, inner_width, comp_count * 2 * freq_local)]
    dot_general x2 -> x0, local copies, waits for them, and re-layouts: 9.46 us -> none  [body(): product = jnp.dot(rows, tile_mats[b], preferred_element_type=jnp.float32)]
    dot_general x5 -> x4, matrix products: 18.5 us -> 10.1 us  [the longest x1 6.9 us: body(): jnp.einsum('sbqi,bix->sbqx', weight_recv, tile_mats, preferred_element_ty...]
  transfers between devices with their start and end apart: 3 -> 3, of which waited for: 1 -> 3; matrix products, arithmetic and copies ran while one was open for 55% -> 27% of each run, Pallas kernels for 0% -> 0%
where the time goes in v2:
time: 110 us; the launch traced here: 109 us
  waiting for transfers between devices  41.5 us (38%)
  local copies, waits for them, and re-layouts  21.2 us (19%)
  other arithmetic  15.1 us (14%)
  starting transfers between devices  15.1 us (14%)
  matrix products  10.1 us (9%)
  Pallas kernels  4.82 us (4%)
    all_to_all x1, waiting for transfers between devices, body(): lax.all_to_all(partial, axes, split_axis=0, concat_axis=0, tiled=True)  20.9 us
    all_to_all x1, waiting for transfers between devices, body(): lax.all_to_all(slip_send, axes, split_axis=0, concat_axis=0, tiled=True)  17.9 us
    reshape x1, local copies, waits for them, and re-layouts, body(): green.reshape(blocks_local, inner_width, comp_count * 2 * freq_local)  11.2 us
    all_to_all x1, starting transfers between devices, body(): lax.all_to_all(weight_send, axes, split_axis=0, concat_axis=0, tiled=True)  7.44 us
    dot_general x1, matrix products, body(): jnp.einsum('sbqi,bix->sbqx', weight_recv, tile_mats, preferred_element_ty...  6.9 us
    pallas_call x1, Pallas kernels, oscillate(): pl.pallas_call(oscillate_kernel, grid=(steps,), in_specs=[whole(spectra.s...  4.82 us
    unnamed x14, local copies, waits for them, and re-layouts  4.4 us
    all_to_all x1, starting transfers between devices, body(): lax.all_to_all(partial, axes, split_axis=0, concat_axis=0, tiled=True)  3.93 us
  transfers between devices with their start and end apart: 3, of which 3 were waited for; matrix products, arithmetic and copies ran while one was open for 27% of the time, Pallas kernels for 0%

profile of v2, /device:TPU:0, one launch (start us, length us, event | category | flops | bytes accessed | tf_op | source)
XLA Modules:
  0.0 108.8 jit_solution(9718971929048454370)
XLA Ops:
  0.7 1.0 copy.25
  1.8 0.8 fusion.105
  2.7 0.9 convolution_convert_fusion.2
  3.6 1.0 broadcast_in_dim.10
  4.6 7.4 %all-to-all-start = ((bf16[32,2,8,768]{3,2,1,0:T(8,128)(2,1)}), bf16[32,2,8,768]{3,2,1,0:T(8,128)(2,1)}, u32[]{:S(2)}, u32[]{:S(2)}) async-start(bf16[32,2,8,768]{3,2,1,0:T(8,128)(2,1)} %bitcast.2), calls=%async_computation | async-start | bytes 1572864 | tf_op jit(solution)/shard_map/all_to_all | solution.py:157
  12.0 11.2 %reshape.234 = bf16[2,768,2048,1]{2,1,0,3:T(8,128)(2,1)} reshape(bf16[2,128,6,2,2,512]{5,4,3,2,1,0:T(2,128)(2,1)} %param.7) | data formatting | bytes 12582912 | tf_op jit(solution)/shard_map/reshape | solution.py:166
  23.2 0.3 reshape.236
  23.6 0.5 copy.28
  24.1 0.5 convolution_convert_fusion
  24.6 1.1 %copy.29 = bf16[16,2,2,2,8,512]{5,4,2,3,1,0:T(8,128)(2,1)} copy(bf16[16,2,2,2,8,512]{5,4,3,1,2,0:T(8,128)(2,1)S(1)} %bitcast.107) | data formatting | bytes 2097152 | tf_op jit(solution)/shard_map/transpose | solution.py:163
  25.7 1.1 %sine_multiply_fusion.1 = (f32[512,128]{1,0:T(8,128)S(1)}, f32[512,128]{1,0:T(8,128)S(1)}) fusion(s32[512]{0:T(512)S(1)} %get-tuple-element.109), kind=kLoop, calls=%fused_computation.79 | loop fusion | flops 1048576 | bytes 526336 | tf_op jit(solution)/shard_map/mul | solution.py:30
  26.9 1.1 %sine_multiply_fusion = (f32[512,128]{1,0:T(8,128)S(1)}, f32[512,128]{1,0:T(8,128)S(1)}) fusion(s32[512]{0:T(512)S(1)} %get-tuple-element.110), kind=kLoop, calls=%fused_computation.67 | loop fusion | flops 1048576 | bytes 526336 | tf_op jit(solution)/shard_map/mul | solution.py:30
  28.3 0.9 fusion.16
  29.9 2.6 %all-to-all-done = bf16[32,2,8,768]{3,2,1,0:T(8,128)(2,1)} async-done(((bf16[32,2,8,768]{3,2,1,0:T(8,128)(2,1)}), bf16[32,2,8,768]{3,2,1,0:T(8,128)(2,1)}, u32[]{:S(2)}, u32[]{:S(2)}) %all-to-all-start) | async-done | bytes 786464 | tf_op jit(solution)/shard_map/all_to_all | solution.py:157
  32.6 3.7 %all-to-all-start.1 = ((bf16[32,2,2,8,512]{4,3,1,2,0:T(8,128)(2,1)}), bf16[32,2,2,8,512]{4,3,1,2,0:T(8,128)(2,1)}, u32[]{:S(2)}, u32[]{:S(2)}) async-start(bf16[32,2,2,8,512]{4,3,1,2,0:T(8,128)(2,1)} %bitcast.106), calls=%async_computation.1 | async-start | bytes 2097152 | tf_op jit(solution)/shard_map/all_to_all | solution.py:165
  36.4 0.3 fusion.54
  37.7 6.9 %fusion.2 = f32[32,2,8,2048]{3,2,0,1:T(8,128)} fusion(bf16[2,768,2048,1]{2,1,0,3:T(8,128)(2,1)} %reshape.234, bf16[32,2,8,768]{3,2,1,0:T(8,128)(2,1)} %all-to-all-done), kind=kOutput, calls=%fused_computation.2 | convolution fusion | flops 1610612736 | bytes 11272192 | tf_op jit(solution)/shard_map/sbqi,bix->sbqx/dot_general | solution.py:167
  44.6 17.9 %all-to-all-done.1 = bf16[32,2,2,8,512]{4,3,1,2,0:T(8,128)(2,1)} async-done(((bf16[32,2,2,8,512]{4,3,1,2,0:T(8,128)(2,1)}), bf16[32,2,2,8,512]{4,3,1,2,0:T(8,128)(2,1)}, u32[]{:S(2)}, u32[]{:S(2)}) %all-to-all-start.1) | async-done | bytes 1048608 | tf_op jit(solution)/shard_map/all_to_all | solution.py:165
  62.5 1.5 %copy_convert_fusion = f32[32,2,2,8,512]{4,3,0,1,2:T(8,128)S(1)} fusion(bf16[32,2,2,8,512]{4,3,1,2,0:T(8,128)(2,1)} %all-to-all-done.1), kind=kLoop, calls=%fused_computation.15 | loop fusion | flops 524288 | bytes 3145728 | tf_op jit(solution)/shard_map/convert_element_type | solution.py:168
  64.0 2.8 %subtract_reduce_fusion.1 = (bf16[32,8,512]{2,1,0:T(8,128)(2,1)S(1)}, bf16[32,8,512]{2,1,0:T(8,128)(2,1)S(1)}, bf16[32,8,512]{2,1,0:T(8,128)(2,1)S(1)}, bf16[32,8,512]{2,1,0:T(8,128)(2,1)S(1)}) fusion(f32[32,2,8,2048]{3,2,0,1:T(8,128)} %fusion.2, f32[32,2,2,8,512]{4,3,0,1,2:T(8,128)S(1)} %copy_convert_fusion), kind=kLoop, calls=%fused_computation.20 | loop fusion | flops 3670016 | bytes 7340032 | tf_op jit(solution)/shard_map/reduce_sum | solution.py:175
  67.0 1.8 %convolution_convert_fusion.1 = bf16[1024,512]{1,0:T(8,128)(2,1)} fusion(bf16[1024,512]{1,0:T(8,128)(2,1)S(1)} %bitcast.111, s32[512]{0:T(512)S(1)} %fusion.106), kind=kOutput, calls=%fused_computation.7 | convolution fusion | flops 537657344 | bytes 2099200 | tf_op jit(solution)/shard_map/dot_general | solution.py:181
  68.8 3.9 %all-to-all-start.2 = ((bf16[32,4,8,512]{3,2,1,0:T(8,128)(2,1)}), bf16[32,4,8,512]{3,2,1,0:T(8,128)(2,1)}, u32[]{:S(2)}, u32[]{:S(2)}) async-start(bf16[32,4,8,512]{3,2,1,0:T(8,128)(2,1)} %bitcast.110), calls=%async_computation.2 | async-start | bytes 2097152 | tf_op jit(solution)/shard_map/all_to_all | solution.py:187
  72.7 1.0 pad_maximum_fusion.1.gain_ref
  75.8 1.0 copy-done
  76.8 1.0 copy-done.2
  77.8 20.9 %all-to-all-done.2 = bf16[32,4,8,512]{3,2,1,0:T(8,128)(2,1)} async-done(((bf16[32,4,8,512]{3,2,1,0:T(8,128)(2,1)}), bf16[32,4,8,512]{3,2,1,0:T(8,128)(2,1)}, u32[]{:S(2)}, u32[]{:S(2)}) %all-to-all-start.2) | async-done | bytes 1048608 | tf_op jit(solution)/shard_map/all_to_all | solution.py:187
  98.7 1.4 %convert_reduce_fusion = f32[2,2,2,8,2,256]{5,3,4,2,1,0:T(8,128)S(1)} fusion(bf16[16,2,2,2,8,2,256]{6,4,5,3,2,1,0:T(8,128)(2,1)} %bitcast.59), kind=kLoop, calls=%fused_computation.6 | loop fusion | flops 1015808 | bytes 1179648 | tf_op jit(solution)/shard_map/reduce_sum | solution.py:191
  100.2 1.2 %copy-done.1 = bf16[512,1024]{1,0:T(8,128)(2,1)S(1)} copy-done((bf16[512,1024]{1,0:T(8,128)(2,1)S(1)}, bf16[512,1024]{1,0:T(8,128)(2,1)}, u32[]{:S(2)}) %copy-start.1) | copy-done | bytes 1048600
  101.4 1.2 %copy-done.3 = bf16[512,1024]{1,0:T(8,128)(2,1)S(1)} copy-done((bf16[512,1024]{1,0:T(8,128)(2,1)S(1)}, bf16[512,1024]{1,0:T(8,128)(2,1)}, u32[]{:S(2)}) %copy-start.3) | copy-done | bytes 1048600
  102.6 4.8 %shard_map.86 = (f32[16,2048]{1,0:T(8,128)S(1)}, f32[4,4,64]{2,1,0:T(4,128)S(1)}) custom-call(f32[2,2,16,512]{3,2,1,0:T(8,128)S(1)} %bitcast.103, f32[2,2,64,512]{3,2,1,0:T(8,128)S(1)} %pad_maximum_fusion.1.gain_ref, bf16[512,1024]{1,0:T(8,128)(2,1)S(1)} %get-tuple-element.43.ce_ref, bf16[512,1024]{1,0:T(8,128)(2,1)S(1)} %copy-done.3, ...), custom_call_target="tpu_custom_call" | custom-call | tf_op jit(solution)/shard_map/pallas_call | solution.py:110
  107.4 0.8 copy.48
  108.2 0.6 copy.49
  (45 shorter events, 4.6 us)
Async XLA Ops:
  4.6 28.0 %all-to-all-start = ((bf16[32,2,8,768]{3,2,1,0:T(8,128)(2,1)}), bf16[32,2,8,768]{3,2,1,0:T(8,128)(2,1)}, u32[]{:S(2)}, u32[]{:S(2)}) async-start(bf16[32,2,8,768]{3,2,1,0:T(8,128)(2,1)} %bitcast.2), calls=%async_computation | async-start | bytes 1572864 | tf_op jit(solution)/shard_map/all_to_all | solution.py:157
  12.0 11.2 %copy-start.4 = (bf16[8,16,2,1024]{3,2,1,0:T(2,128)(2,1)S(1)}, bf16[8,16,2,1024]{3,2,1,0:T(2,128)(2,1)}, u32[]{:S(2)}) copy-start(bf16[8,16,2,1024]{3,2,1,0:T(2,128)(2,1)} %param.9) | copy-start | bytes 1572868
  24.1 4.1 %copy-start.5 = (f32[64]{0:T(128)S(1)}, f32[64]{0:T(128)}, u32[]{:S(2)}) copy-start(f32[64]{0:T(128)} %param.12) | copy-start | bytes 772
  24.1 4.1 %copy-start.6 = (f32[64]{0:T(128)S(1)}, f32[64]{0:T(128)}, u32[]{:S(2)}) copy-start(f32[64]{0:T(128)} %param.13) | copy-start | bytes 772
  32.6 29.9 %all-to-all-start.1 = ((bf16[32,2,2,8,512]{4,3,1,2,0:T(8,128)(2,1)}), bf16[32,2,2,8,512]{4,3,1,2,0:T(8,128)(2,1)}, u32[]{:S(2)}, u32[]{:S(2)}) async-start(bf16[32,2,2,8,512]{4,3,1,2,0:T(8,128)(2,1)} %bitcast.106), calls=%async_computation.1 | async-start | bytes 2097152 | tf_op jit(solution)/shard_map/all_to_all | solution.py:165
  68.8 29.9 %all-to-all-start.2 = ((bf16[32,4,8,512]{3,2,1,0:T(8,128)(2,1)}), bf16[32,4,8,512]{3,2,1,0:T(8,128)(2,1)}, u32[]{:S(2)}, u32[]{:S(2)}) async-start(bf16[32,4,8,512]{3,2,1,0:T(8,128)(2,1)} %bitcast.110), calls=%async_computation.2 | async-start | bytes 2097152 | tf_op jit(solution)/shard_map/all_to_all | solution.py:187
  75.8 1.0 copy-start
  76.8 1.0 copy-start.2
  100.2 1.2 %copy-start.1 = (bf16[512,1024]{1,0:T(8,128)(2,1)S(1)}, bf16[512,1024]{1,0:T(8,128)(2,1)}, u32[]{:S(2)}) copy-start(bf16[512,1024]{1,0:T(8,128)(2,1)} %copy-done) | copy-start | bytes 3145732
  101.4 1.2 %copy-start.3 = (bf16[512,1024]{1,0:T(8,128)(2,1)S(1)}, bf16[512,1024]{1,0:T(8,128)(2,1)}, u32[]{:S(2)}) copy-start(bf16[512,1024]{1,0:T(8,128)(2,1)} %copy-done.2) | copy-start | bytes 3145732

commit v3 on v2

--- a/solution.py
+++ b/solution.py
@@ -150,11 +150,13 @@
     weight_rows = slip_weights.transpose(0, 1, 3, 2).reshape(slot_rows, inner_width)
     weight_rows = jnp.dot(weight_rows, turn, preferred_element_type=f32).astype(bf16)
     weight_send = jnp.dot(pick, weight_rows, preferred_element_type=f32).astype(bf16)
-    weight_send = jnp.broadcast_to(
-        weight_send.reshape(fault_count, 1, blocks_local, owned_count, inner_width),
-        (fault_count, group_size, blocks_local, owned_count, inner_width),
-    ).reshape(device_count, blocks_local, owned_count, inner_width)
-    weight_recv = lax.all_to_all(weight_send, axes, split_axis=0, concat_axis=0, tiled=True)
+    weight_send = weight_send.reshape(fault_count, blocks_local, owned_count, inner_width)
+    weight_own = lax.all_to_all(weight_send, "fault", split_axis=0, concat_axis=0, tiled=True)
+    rup = lax.axis_index("rup")
+    weight_recv = [weight_own]
+    for shift in range(1, group_size):
+        ring = [(i, (i + shift) % group_size) for i in range(group_size)]
+        weight_recv.append(lax.ppermute(weight_own, "rup", ring))
     slip_rows = slip_spectra.reshape(slot_rows, 2, group_size, freq_local).transpose(0, 2, 1, 3)
     slip_rows = slip_rows.reshape(slot_rows, 2 * freq_count)
     slip_send = jnp.dot(pick, slip_rows, preferred_element_type=f32).astype(bf16)
@@ -164,7 +166,18 @@
     slip_send = slip_send.reshape(device_count, blocks_local, 2, owned_count, freq_local)
     slip_recv = lax.all_to_all(slip_send, axes, split_axis=0, concat_axis=0, tiled=True)
     tile_mats = green.reshape(blocks_local, inner_width, comp_count * 2 * freq_local)
-    product = jnp.einsum("sbqi,bix->sbqx", weight_recv, tile_mats, preferred_element_type=f32)
+    weight_all = jnp.stack(
+        [
+            lax.select_n((rup - g) % group_size, *weight_recv)
+            if group_size == 2
+            else lax.dynamic_index_in_dim(
+                jnp.stack(weight_recv), (rup - g) % group_size, 0, keepdims=False
+            )
+            for g in range(group_size)
+        ],
+        axis=1,
+    ).reshape(device_count, blocks_local, owned_count, inner_width)
+    product = jnp.einsum("sbqi,bix->sbqx", weight_all, tile_mats, preferred_element_type=f32)
     slip_f = slip_recv.astype(f32)
     ones = []
     for c in range(comp_count):

time: 110 us -> 105 us (0.955)
  waiting for transfers between devices: 41.5 us -> 27.8 us
  starting transfers between devices: 15.1 us -> 18.6 us
  other arithmetic: 15.1 us -> 17.6 us
  local copies, waits for them, and re-layouts: 21.2 us -> 23.7 us
    all_to_all x1, waiting for transfers between devices: 17.9 us -> 0.01 us  [body(): lax.all_to_all(slip_send, axes, split_axis=0, concat_axis=0, tiled=True)]
    ppermute x0 -> x1, waiting for transfers between devices: none -> 4.36 us  [body(): weight_recv.append(lax.ppermute(weight_own, 'rup', ring))]
    slice x4, local copies, waits for them, and re-layouts: 0.06 us -> 3.45 us  [half_tables(): ca, sa = (cos_c[:, a:a + 1], sin_c[:, a:a + 1])]
    all_to_all x1, starting transfers between devices: 3.93 us -> 5.92 us  [body(): lax.all_to_all(partial, axes, split_axis=0, concat_axis=0, tiled=True)]
    ppermute x0 -> x1, starting transfers between devices: none -> 1.76 us  [body(): weight_recv.append(lax.ppermute(weight_own, 'rup', ring))]
    another operation x0 -> x2, other arithmetic: none -> 1.13 us  [body(): jnp.stack([lax.select_n((rup - g) % group_size, *weight_recv) if group_si...]
    unnamed x14 -> x56, local copies, waits for them, and re-layouts: 4.4 us -> 4.47 us
  transfers between devices with their start and end apart: 3 -> 4, of which waited for: 3 -> 3; matrix products, arithmetic and copies ran while one was open for 27% -> 33% of each run, Pallas kernels for 0% -> 0%
where the time goes in v3:
time: 105 us; the launch traced here: 104 us
  waiting for transfers between devices  27.8 us (26%)
  local copies, waits for them, and re-layouts  23.7 us (23%)
  starting transfers between devices  18.6 us (18%)
  other arithmetic  17.6 us (17%)
  matrix products  10.6 us (10%)
  Pallas kernels  4.73 us (5%)
  between operations  1.25 us (1%)
    all_to_all x1, waiting for transfers between devices, body(): lax.all_to_all(partial, axes, split_axis=0, concat_axis=0, tiled=True)  20.7 us
    reshape x1, local copies, waits for them, and re-layouts, body(): green.reshape(blocks_local, inner_width, comp_count * 2 * freq_local)  11.1 us
    all_to_all x1, starting transfers between devices, body(): lax.all_to_all(weight_send, 'fault', split_axis=0, concat_axis=0, tiled=T...  7.39 us
    dot_general x1, matrix products, body(): jnp.einsum('sbqi,bix->sbqx', weight_all, tile_mats, preferred_element_typ...  6.68 us
    all_to_all x1, starting transfers between devices, body(): lax.all_to_all(partial, axes, split_axis=0, concat_axis=0, tiled=True)  5.92 us
    pallas_call x1, Pallas kernels, oscillate(): pl.pallas_call(oscillate_kernel, grid=(steps,), in_specs=[whole(spectra.s...  4.73 us
    unnamed x56, local copies, waits for them, and re-layouts  4.47 us
    ppermute x1, waiting for transfers between devices, body(): weight_recv.append(lax.ppermute(weight_own, 'rup', ring))  4.36 us
  transfers between devices with their start and end apart: 4, of which 3 were waited for; matrix products, arithmetic and copies ran while one was open for 33% of the time, Pallas kernels for 0%

profile of v3, /device:TPU:0, one launch (start us, length us, event | category | flops | bytes accessed | tf_op | source)
XLA Modules:
  0.0 104.3 jit_solution(5425495003465258101)
XLA Ops:
  0.7 1.0 %copy.25 = bf16[8,16,6,128]{3,2,1,0:T(8,128)(2,1)S(1)} copy(bf16[8,16,6,128]{3,1,2,0:T(8,128)(2,1)} %bitcast.124) | data formatting | bytes 393216 | tf_op jit(solution)/shard_map/transpose | solution.py:150
  1.8 0.8 fusion.104
  2.8 1.6 %convolution_convert_fusion.2 = bf16[256,768]{1,0:T(8,128)(2,1)} fusion(s32[768]{0:T(1024)S(1)} %fusion.97, bf16[16,8,6,128]{3,2,1,0:T(8,128)(2,1)S(1)} %bitcast.123, s32[128]{0:T(128)S(1)} %get-tuple-element.107, s32[128]{0:T(128)S(1)} %get-tuple-element.108, s32[256]{0:T(256)S(1)} %iota.116, s32[128]{0:T(128)S(1)} %eq.54, s32[256]{0:T(256)S(1)} %iota.113, ...), kind=kOutput, calls=%fused_computation.8 | convolution fusion | flops 202932224 | bytes 596608 | tf_op jit(solution)/shard_map/dot_general | solution.py:152
  4.4 7.4 %all-to-all-start = ((bf16[16,2,8,768]{3,2,1,0:T(8,128)(2,1)}), bf16[16,2,8,768]{3,2,1,0:T(8,128)(2,1)S(1)}, u32[]{:S(2)}, u32[]{:S(2)}) async-start(bf16[16,2,8,768]{3,2,1,0:T(8,128)(2,1)} %bitcast.1), calls=%async_computation | async-start | bytes 786432 | tf_op jit(solution)/shard_map/all_to_all | solution.py:154
  13.3 1.1 %sine_multiply_fusion.1 = (f32[512,128]{1,0:T(8,128)S(1)}, f32[512,128]{1,0:T(8,128)S(1)}) fusion(s32[512]{0:T(512)S(1)} %get-tuple-element.111), kind=kLoop, calls=%fused_computation.81 | loop fusion | flops 1048576 | bytes 526336 | tf_op jit(solution)/shard_map/mul | solution.py:30
  14.4 0.8 fusion.87
  17.2 1.0 fusion.15
  18.2 1.1 %sine_multiply_fusion = (f32[512,128]{1,0:T(8,128)S(1)}, f32[512,128]{1,0:T(8,128)S(1)}) fusion(s32[512]{0:T(512)S(1)} %copy-done.7), kind=kLoop, calls=%fused_computation.69 | loop fusion | flops 1048576 | bytes 526336 | tf_op jit(solution)/shard_map/mul | solution.py:30
  19.3 1.1 %copy.29 = bf16[16,2,2,2,8,512]{5,4,2,3,1,0:T(8,128)(2,1)} copy(bf16[16,2,2,2,8,512]{5,4,3,1,2,0:T(8,128)(2,1)S(1)} %bitcast.113) | data formatting | bytes 2097152 | tf_op jit(solution)/shard_map/transpose | solution.py:165
  21.2 2.8 %all-to-all-done = bf16[16,2,8,768]{3,2,1,0:T(8,128)(2,1)S(1)} async-done(((bf16[16,2,8,768]{3,2,1,0:T(8,128)(2,1)}), bf16[16,2,8,768]{3,2,1,0:T(8,128)(2,1)S(1)}, u32[]{:S(2)}, u32[]{:S(2)}) %all-to-all-start) | async-done | bytes 393248 | tf_op jit(solution)/shard_map/all_to_all | solution.py:154
  24.0 3.5 %all-to-all-start.1 = ((bf16[32,2,2,8,512]{4,3,1,2,0:T(8,128)(2,1)}), bf16[32,2,2,8,512]{4,3,1,2,0:T(8,128)(2,1)}, u32[]{:S(2)}, u32[]{:S(2)}) async-start(bf16[32,2,2,8,512]{4,3,1,2,0:T(8,128)(2,1)} %bitcast.112), calls=%async_computation.1 | async-start | bytes 2097152 | tf_op jit(solution)/shard_map/all_to_all | solution.py:167
  27.5 1.6 %fusion.113 = (f32[512,1]{0,1:T(1,128)}, f32[512,1]{0,1:T(1,128)}, f32[512,1]{0,1:T(1,128)}, f32[512,1]{0,1:T(1,128)}, f32[512,1]{0,1:T(1,128)}, /*index=5*/f32[...) fusion(f32[512,8]{0,1:T(8,128)} %get-tuple-element.18), kind=kLoop, calls=%fused_computation.203 | loop fusion | bytes 32768 | tf_op jit(solution)/shard_map/slice | solution.py:34
  29.1 0.9 fusion.56
  30.0 1.8 %collective-permute-start = (bf16[16,2,8,768]{3,2,1,0:T(8,128)(2,1)S(1)}, bf16[16,2,8,768]{3,2,1,0:T(8,128)(2,1)}, u32[]{:S(2)}, u32[]{:S(2)}) collective-permute-start(bf16[16,2,8,768]{3,2,1,0:T(8,128)(2,1)S(1)} %all-to-all-done), channel_id=1, source_target_pairs={{0,1},{1,0},{2,3},{3,2},{4,5},{5,4},{6,7},{7,6},{8,9},{9,8},{10,11... | collective-permute-start | bytes 1179656 | tf_op jit(solution)/shard_map/ppermute | solution.py:159
  31.8 0.6 fusion.112
  32.4 11.1 %reshape.236 = bf16[2,768,2048,1]{2,1,0,3:T(8,128)(2,1)} reshape(bf16[2,128,6,2,2,512]{5,4,3,2,1,0:T(2,128)(2,1)} %param.7) | data formatting | bytes 12582912 | tf_op jit(solution)/shard_map/reshape | solution.py:168
  43.8 4.4 %collective-permute-done = bf16[16,2,8,768]{3,2,1,0:T(8,128)(2,1)} collective-permute-done((bf16[16,2,8,768]{3,2,1,0:T(8,128)(2,1)S(1)}, bf16[16,2,8,768]{3,2,1,0:T(8,128)(2,1)}, u32[]{:S(2)}, u32[]{:S(2)}) %collective-permute-start) | collective-permute-done | bytes 393248 | tf_op jit(solution)/shard_map/ppermute | solution.py:159
  48.2 1.1 %select_bitcast_fusion.1 = (bf16[16,1,2,8,768]{4,3,2,0,1:T(8,128)(2,1)S(1)}, bf16[16,1,2,8,768]{4,3,2,0,1:T(8,128)(2,1)S(1)}) fusion(bf16[16,2,8,768]{3,2,1,0:T(8,128)(2,1)S(1)} %all-to-all-done, bf16[16,2,8,768]{3,2,1,0:T(8,128)(2,1)} %collective-permute-done, pred[]{:T(512)S(6)} %select_n.106, pred[]{:T(512)S(6)} %select_n.114), kind=kLoop, calls=%fused_computation.31 | loop fusion | flops 393216 | bytes 1572866 | tf_op jit(solution)/shard_map/stack | solution.py:169
  49.4 6.7 %fusion.2 = f32[32,2,8,2048]{3,2,0,1:T(8,128)} fusion(bf16[32,2,8,768]{3,2,0,1:T(8,128)(2,1)S(1)} %bitcast.111, bf16[2,768,2048,1]{2,1,0,3:T(8,128)(2,1)} %reshape.236), kind=kOutput, calls=%fused_computation.2 | convolution fusion | flops 1610612736 | bytes 11272192 | tf_op jit(solution)/shard_map/sbqi,bix->sbqx/dot_general | solution.py:180
  56.1 1.5 %copy_convert_fusion = f32[32,2,2,8,512]{4,3,0,1,2:T(8,128)S(1)} fusion(bf16[32,2,2,8,512]{4,3,1,2,0:T(8,128)(2,1)} %all-to-all-done.1), kind=kLoop, calls=%fused_computation.15 | loop fusion | flops 524288 | bytes 3145728 | tf_op jit(solution)/shard_map/convert_element_type | solution.py:181
  57.6 2.8 %subtract_reduce_fusion.1 = (bf16[32,8,512]{2,1,0:T(8,128)(2,1)S(1)}, bf16[32,8,512]{2,1,0:T(8,128)(2,1)S(1)}, bf16[32,8,512]{2,1,0:T(8,128)(2,1)S(1)}, bf16[32,8,512]{2,1,0:T(8,128)(2,1)S(1)}) fusion(f32[32,2,8,2048]{3,2,0,1:T(8,128)} %fusion.2, f32[32,2,2,8,512]{4,3,0,1,2:T(8,128)S(1)} %copy_convert_fusion), kind=kLoop, calls=%fused_computation.20 | loop fusion | flops 3670016 | bytes 7340032 | tf_op jit(solution)/shard_map/reduce_sum | solution.py:188
  60.5 1.8 %convolution_convert_fusion.1 = bf16[1024,512]{1,0:T(8,128)(2,1)} fusion(bf16[1024,512]{1,0:T(8,128)(2,1)S(1)} %bitcast.117, s32[512]{0:T(512)S(1)} %fusion.105), kind=kOutput, calls=%fused_computation.7 | convolution fusion | flops 537657344 | bytes 2099200 | tf_op jit(solution)/shard_map/dot_general | solution.py:194
  62.4 5.9 %all-to-all-start.2 = ((bf16[32,4,8,512]{3,2,1,0:T(8,128)(2,1)}), bf16[32,4,8,512]{3,2,1,0:T(8,128)(2,1)}, u32[]{:S(2)}, u32[]{:S(2)}) async-start(bf16[32,4,8,512]{3,2,1,0:T(8,128)(2,1)} %bitcast.116), calls=%async_computation.2 | async-start | bytes 2097152 | tf_op jit(solution)/shard_map/all_to_all | solution.py:200
  68.4 1.0 pad_maximum_fusion.2.gain_ref
  71.7 1.0 copy-done
  72.7 1.0 copy-done.2
  73.6 20.7 %all-to-all-done.2 = bf16[32,4,8,512]{3,2,1,0:T(8,128)(2,1)} async-done(((bf16[32,4,8,512]{3,2,1,0:T(8,128)(2,1)}), bf16[32,4,8,512]{3,2,1,0:T(8,128)(2,1)}, u32[]{:S(2)}, u32[]{:S(2)}) %all-to-all-start.2) | async-done | bytes 1048608 | tf_op jit(solution)/shard_map/all_to_all | solution.py:200
  94.3 1.4 %convert_reduce_fusion = f32[2,2,2,8,2,256]{5,3,4,2,1,0:T(8,128)S(1)} fusion(bf16[16,2,2,2,8,2,256]{6,4,5,3,2,1,0:T(8,128)(2,1)} %bitcast.61), kind=kLoop, calls=%fused_computation.6 | loop fusion | flops 1015808 | bytes 1179648 | tf_op jit(solution)/shard_map/reduce_sum | solution.py:204
  95.8 1.2 %copy-done.1 = bf16[512,1024]{1,0:T(8,128)(2,1)S(1)} copy-done((bf16[512,1024]{1,0:T(8,128)(2,1)S(1)}, bf16[512,1024]{1,0:T(8,128)(2,1)}, u32[]{:S(2)}) %copy-start.1) | copy-done | bytes 1048600
  97.0 1.2 %copy-done.3 = bf16[512,1024]{1,0:T(8,128)(2,1)S(1)} copy-done((bf16[512,1024]{1,0:T(8,128)(2,1)S(1)}, bf16[512,1024]{1,0:T(8,128)(2,1)}, u32[]{:S(2)}) %copy-start.3) | copy-done | bytes 1048600
  98.2 4.7 %shard_map.86 = (f32[16,2048]{1,0:T(8,128)S(1)}, f32[4,4,64]{2,1,0:T(4,128)S(1)}) custom-call(f32[2,2,16,512]{3,2,1,0:T(8,128)S(1)} %bitcast.108, f32[2,2,64,512]{3,2,1,0:T(8,128)S(1)} %pad_maximum_fusion.2.gain_ref, bf16[512,1024]{1,0:T(8,128)(2,1)S(1)} %get-tuple-element.45.ce_ref, bf16[512,1024]{1,0:T(8,128)(2,1)S(1)} %copy-done.3, ...), custom_call_target="tpu_custom_call" | custom-call | tf_op jit(solution)/shard_map/pallas_call | solution.py:110
  103.0 0.8 copy.46
  (91 shorter events, 7.7 us)
Async XLA Ops:
  0.6 11.2 %copy-start.5 = (bf16[8,16,2,1024]{3,2,1,0:T(2,128)(2,1)S(1)}, bf16[8,16,2,1024]{3,2,1,0:T(2,128)(2,1)}, u32[]{:S(2)}) copy-start(bf16[8,16,2,1024]{3,2,1,0:T(2,128)(2,1)} %param.9) | copy-start | bytes 1572868
  4.4 19.6 %all-to-all-start = ((bf16[16,2,8,768]{3,2,1,0:T(8,128)(2,1)}), bf16[16,2,8,768]{3,2,1,0:T(8,128)(2,1)S(1)}, u32[]{:S(2)}, u32[]{:S(2)}) async-start(bf16[16,2,8,768]{3,2,1,0:T(8,128)(2,1)} %bitcast.1), calls=%async_computation | async-start | bytes 786432 | tf_op jit(solution)/shard_map/all_to_all | solution.py:154
  11.8 4.6 %copy-start.26 = (f32[64]{0:T(128)S(1)}, f32[64]{0:T(128)}, u32[]{:S(2)}) copy-start(f32[64]{0:T(128)} %param.12) | copy-start | bytes 772
  11.8 4.6 %copy-start.27 = (f32[64]{0:T(128)S(1)}, f32[64]{0:T(128)}, u32[]{:S(2)}) copy-start(f32[64]{0:T(128)} %param.13) | copy-start | bytes 772
  11.9 4.6 %copy-start.6 = (s32[512]{0:T(512)}, s32[512]{0:T(512)S(1)}, u32[]{:S(2)}) copy-start(s32[512]{0:T(512)S(1)} %get-tuple-element.112) | copy-start | bytes 6148
  16.4 1.7 %copy-start.7 = (s32[512]{0:T(512)S(1)}, s32[512]{0:T(512)}, u32[]{:S(2)}) copy-start(s32[512]{0:T(512)} %copy-done.6) | copy-start | bytes 6148
  24.0 32.1 %all-to-all-start.1 = ((bf16[32,2,2,8,512]{4,3,1,2,0:T(8,128)(2,1)}), bf16[32,2,2,8,512]{4,3,1,2,0:T(8,128)(2,1)}, u32[]{:S(2)}, u32[]{:S(2)}) async-start(bf16[32,2,2,8,512]{4,3,1,2,0:T(8,128)(2,1)} %bitcast.112), calls=%async_computation.1 | async-start | bytes 2097152 | tf_op jit(solution)/shard_map/all_to_all | solution.py:167
  30.0 18.1 %collective-permute-start = (bf16[16,2,8,768]{3,2,1,0:T(8,128)(2,1)S(1)}, bf16[16,2,8,768]{3,2,1,0:T(8,128)(2,1)}, u32[]{:S(2)}, u32[]{:S(2)}) collective-permute-start(bf16[16,2,8,768]{3,2,1,0:T(8,128)(2,1)S(1)} %all-to-all-done), channel_id=1, source_target_pairs={{0,1},{1,0},{2,3},{3,2},{4,5},{5,4},{6,7},{7,6},{8,9},{9,8},{10,11... | collective-permute-start | bytes 1179656 | tf_op jit(solution)/shard_map/ppermute | solution.py:159
  32.4 11.1 %copy-start.11 = (f32[512,1]{0,1:T(1,128)S(1)}, f32[512,1]{0,1:T(1,128)}, u32[]{:S(2)}) copy-start(f32[512,1]{0,1:T(1,128)} %get-tuple-element.84) | copy-start | bytes 6148
  32.4 11.1 %copy-start.14 = (f32[512,1]{0,1:T(1,128)S(1)}, f32[512,1]{0,1:T(1,128)}, u32[]{:S(2)}) copy-start(f32[512,1]{0,1:T(1,128)} %get-tuple-element.76) | copy-start | bytes 6148
  60.5 7.8 %copy-start.4 = (f32[1,2,64,512]{3,2,1,0:T(8,128)S(1)}, f32[1,2,64,512]{3,2,1,0:T(8,128)}, u32[]{:S(2)}) copy-start(f32[1,2,64,512]{3,2,1,0:T(8,128)} %get-tuple-element.92) | copy-start | bytes 786436
  60.5 8.8 %copy-start.21 = (f32[512,1]{0,1:T(1,128)S(1)}, f32[512,1]{0,1:T(1,128)}, u32[]{:S(2)}) copy-start(f32[512,1]{0,1:T(1,128)} %get-tuple-element.75) | copy-start | bytes 6148
  60.5 8.8 %copy-start.25 = (f32[512,1]{0,1:T(1,128)S(1)}, f32[512,1]{0,1:T(1,128)}, u32[]{:S(2)}) copy-start(f32[512,1]{0,1:T(1,128)} %get-tuple-element.67) | copy-start | bytes 6148
  62.4 7.3 %copy-start.19 = (f32[512,1]{0,1:T(1,128)S(1)}, f32[512,1]{0,1:T(1,128)}, u32[]{:S(2)}) copy-start(f32[512,1]{0,1:T(1,128)} %get-tuple-element.74) | copy-start | bytes 6148
  62.4 7.3 %copy-start.24 = (f32[512,1]{0,1:T(1,128)S(1)}, f32[512,1]{0,1:T(1,128)}, u32[]{:S(2)}) copy-start(f32[512,1]{0,1:T(1,128)} %get-tuple-element.66) | copy-start | bytes 6148
  62.4 7.6 %copy-start.17 = (f32[512,1]{0,1:T(1,128)S(1)}, f32[512,1]{0,1:T(1,128)}, u32[]{:S(2)}) copy-start(f32[512,1]{0,1:T(1,128)} %get-tuple-element.73) | copy-start | bytes 6148
  62.4 7.6 %copy-start.23 = (f32[512,1]{0,1:T(1,128)S(1)}, f32[512,1]{0,1:T(1,128)}, u32[]{:S(2)}) copy-start(f32[512,1]{0,1:T(1,128)} %get-tuple-element.65) | copy-start | bytes 6148
  62.4 7.9 %copy-start.15 = (f32[512,1]{0,1:T(1,128)S(1)}, f32[512,1]{0,1:T(1,128)}, u32[]{:S(2)}) copy-start(f32[512,1]{0,1:T(1,128)} %get-tuple-element.72) | copy-start | bytes 6148
  62.4 7.9 %copy-start.22 = (f32[512,1]{0,1:T(1,128)S(1)}, f32[512,1]{0,1:T(1,128)}, u32[]{:S(2)}) copy-start(f32[512,1]{0,1:T(1,128)} %get-tuple-element.64) | copy-start | bytes 6148
  62.4 31.9 %all-to-all-start.2 = ((bf16[32,4,8,512]{3,2,1,0:T(8,128)(2,1)}), bf16[32,4,8,512]{3,2,1,0:T(8,128)(2,1)}, u32[]{:S(2)}, u32[]{:S(2)}) async-start(bf16[32,4,8,512]{3,2,1,0:T(8,128)(2,1)} %bitcast.116), calls=%async_computation.2 | async-start | bytes 2097152 | tf_op jit(solution)/shard_map/all_to_all | solution.py:200
  68.3 2.2 %copy-start.13 = (f32[512,1]{0,1:T(1,128)S(1)}, f32[512,1]{0,1:T(1,128)}, u32[]{:S(2)}) copy-start(f32[512,1]{0,1:T(1,128)} %get-tuple-element.71) | copy-start | bytes 6148
  68.3 2.2 %copy-start.20 = (f32[512,1]{0,1:T(1,128)S(1)}, f32[512,1]{0,1:T(1,128)}, u32[]{:S(2)}) copy-start(f32[512,1]{0,1:T(1,128)} %get-tuple-element.63) | copy-start | bytes 6148
  68.4 2.5 %copy-start.10 = (f32[512,1]{0,1:T(1,128)S(1)}, f32[512,1]{0,1:T(1,128)}, u32[]{:S(2)}) copy-start(f32[512,1]{0,1:T(1,128)} %get-tuple-element.70) | copy-start | bytes 6148
  68.4 2.5 %copy-start.18 = (f32[512,1]{0,1:T(1,128)S(1)}, f32[512,1]{0,1:T(1,128)}, u32[]{:S(2)}) copy-start(f32[512,1]{0,1:T(1,128)} %get-tuple-element.62) | copy-start | bytes 6148
  69.4 1.7 %copy-start.9 = (f32[512,1]{0,1:T(1,128)S(1)}, f32[512,1]{0,1:T(1,128)}, u32[]{:S(2)}) copy-start(f32[512,1]{0,1:T(1,128)} %get-tuple-element.69) | copy-start | bytes 6148
  69.4 1.7 %copy-start.16 = (f32[512,1]{0,1:T(1,128)S(1)}, f32[512,1]{0,1:T(1,128)}, u32[]{:S(2)}) copy-start(f32[512,1]{0,1:T(1,128)} %get-tuple-element.61) | copy-start | bytes 6148
  69.6 1.8 %copy-start.8 = (f32[512,1]{0,1:T(1,128)S(1)}, f32[512,1]{0,1:T(1,128)}, u32[]{:S(2)}) copy-start(f32[512,1]{0,1:T(1,128)} %get-tuple-element.68) | copy-start | bytes 6148
  69.6 1.8 %copy-start.12 = (f32[512,1]{0,1:T(1,128)S(1)}, f32[512,1]{0,1:T(1,128)}, u32[]{:S(2)}) copy-start(f32[512,1]{0,1:T(1,128)} %get-tuple-element.60) | copy-start | bytes 6148
  71.7 1.0 copy-start
  72.7 1.0 copy-start.2
  95.8 1.2 %copy-start.1 = (bf16[512,1024]{1,0:T(8,128)(2,1)S(1)}, bf16[512,1024]{1,0:T(8,128)(2,1)}, u32[]{:S(2)}) copy-start(bf16[512,1024]{1,0:T(8,128)(2,1)} %copy-done) | copy-start | bytes 3145732
  97.0 1.2 %copy-start.3 = (bf16[512,1024]{1,0:T(8,128)(2,1)S(1)}, bf16[512,1024]{1,0:T(8,128)(2,1)}, u32[]{:S(2)}) copy-start(bf16[512,1024]{1,0:T(8,128)(2,1)} %copy-done.2) | copy-start | bytes 3145732

commit v4 on v3

--- a/solution.py
+++ b/solution.py
@@ -122,6 +122,104 @@
         compiler_params=pltpu.CompilerParams(vmem_limit_bytes=40 << 20),
     )(spectra, gain, *tables)
     return wave, peak
+
+
+def plane_width(fault_count):
+    return 2 ** ((fault_count.bit_length() - 1) // 2)
+
+
+def collect_kernel(planes, inner, in_ref, out_ref, near, held, far, near_send, near_recv, far_send, far_recv):
+    mesh_type = pl.DeviceIdType.MESH
+    f32 = jnp.float32
+    group = out_ref.shape[0]
+    members = inner * group
+    fault, rup = lax.axis_index("fault"), lax.axis_index("rup")
+    plane, place = fault // inner, fault % inner
+    member = place * group + rup
+
+    def mate(d):
+        other = (member + d) % members
+        return other, (plane * inner + other // group, other % group)
+
+    def across(dz):
+        other = (plane + dz) % planes
+        return other, (other * inner + place, rup)
+
+    barrier = pltpu.get_barrier_semaphore()
+    for d in range(1, members):
+        pl.semaphore_signal(barrier, inc=1, device_id=mate(d)[1], device_id_type=mesh_type)
+    for dz in range(1, planes):
+        pl.semaphore_signal(barrier, inc=1, device_id=across(dz)[1], device_id_type=mesh_type)
+    pl.semaphore_wait(barrier, members + planes - 2)
+
+    near_copies, far_copies = {}, {}
+    for dz in range(1, planes + 1):
+        target = (plane + dz) % planes
+        for d in range(1, members):
+            other, device = mate(d)
+            near_copies[dz, d] = pltpu.make_async_remote_copy(
+                src_ref=in_ref.at[target, other],
+                dst_ref=near.at[dz - 1, d - 1],
+                send_sem=near_send.at[dz - 1, d - 1],
+                recv_sem=near_recv.at[dz - 1, d - 1],
+                device_id=device,
+                device_id_type=mesh_type,
+            )
+            near_copies[dz, d].start()
+    for dz in range(1, planes + 1):
+        target = (plane + dz) % planes
+        for d in range(1, members):
+            near_copies[dz, d].wait_recv()
+        for k in range(group):
+            terms = [near[dz - 1, d - 1].astype(f32) for d in range(1, members) if d % group == k]
+            if k == 0:
+                terms.append(in_ref[target, member].astype(f32))
+            total = sum(terms[1:], terms[0])
+            if dz < planes:
+                held[dz - 1, k] = total.astype(held.dtype)
+            else:
+                out_ref[k] = total
+        if dz < planes:
+            far_copies[dz] = pltpu.make_async_remote_copy(
+                src_ref=held.at[dz - 1],
+                dst_ref=far.at[dz - 1],
+                send_sem=far_send.at[dz - 1],
+                recv_sem=far_recv.at[dz - 1],
+                device_id=across(dz)[1],
+                device_id_type=mesh_type,
+            )
+            far_copies[dz].start()
+    for dz in range(1, planes):
+        far_copies[dz].wait_recv()
+        out_ref[...] += far[dz - 1].astype(f32)
+    for copy in list(near_copies.values()) + list(far_copies.values()):
+        copy.wait_send()
+
+
+def collect(partial, fault_count, group):
+    inner = plane_width(fault_count)
+    planes, members = fault_count // inner, inner * group
+    rows, width = partial.shape[1:]
+    vmem = pl.BlockSpec(memory_space=pltpu.VMEM)
+    dma = pltpu.SemaphoreType.DMA
+    return pl.pallas_call(
+        lambda *refs: collect_kernel(planes, inner, *refs),
+        in_specs=[vmem],
+        out_specs=vmem,
+        out_shape=jax.ShapeDtypeStruct((group, rows, width), jnp.float32),
+        scratch_shapes=[
+            pltpu.VMEM((planes, members - 1, rows, width), partial.dtype),
+            pltpu.VMEM((planes - 1, group, rows, width), partial.dtype),
+            pltpu.VMEM((planes - 1, group, rows, width), partial.dtype),
+            dma((planes, members - 1)),
+            dma((planes, members - 1)),
+            dma((planes - 1,)),
+            dma((planes - 1,)),
+        ],
+        compiler_params=pltpu.CompilerParams(
+            collective_id=0, has_side_effects=True, vmem_limit_bytes=16 << 20
+        ),
+    )(partial.reshape(planes, members, rows, width))
 
 
 def body(green, slip_weights, slip_spectra, block_lists, block_counts, natural_freq, damping):
@@ -196,12 +294,18 @@
         deal,
         preferred_element_type=f32,
     ).astype(bf16)
-    partial = partial.reshape(device_count, comp_count * 2, owned_count, freq_local)
-    returned = lax.all_to_all(partial, axes, split_axis=0, concat_axis=0, tiled=True)
-    returned = returned.reshape(
-        fault_count, group_size, comp_count, 2, owned_count, 2, freq_local // 2
-    ).astype(f32)
-    spectra = jnp.sum(returned, axis=0).transpose(2, 4, 1, 3, 0, 5)
+    partial = partial.reshape(device_count, comp_count * 2 * owned_count, freq_local)
+    shares = collect(partial, fault_count, group_size)
+    shares = jnp.stack(
+        [
+            lax.select_n((rup - g) % group_size, shares[0], shares[1])
+            if group_size == 2
+            else lax.dynamic_index_in_dim(shares, (rup - g) % group_size, 0, keepdims=False)
+            for g in range(group_size)
+        ]
+    )
+    shares = shares.reshape(group_size, comp_count, 2, owned_count, 2, freq_local // 2)
+    spectra = shares.transpose(2, 4, 1, 3, 0, 5)
     spectra = spectra.reshape(2, 2, comp_count * owned_count, freq_count // 2)
     gain = split_gain(natural_freq, damping, freq_count)
     tables = half_tables(freq_count)

time: 105 us -> 89.3 us (0.85)
  waiting for transfers between devices: 27.8 us -> 4.25 us
  Pallas kernels: 4.73 us -> 24.8 us
  local copies, waits for them, and re-layouts: 23.7 us -> 15.9 us
  matrix products: 10.6 us -> 6.81 us
  starting transfers between devices: 18.6 us -> 15.2 us
  other arithmetic: 17.6 us -> 20.7 us
    all_to_all x1 -> x0, waiting for transfers between devices: 20.7 us -> none  [body(): lax.all_to_all(partial, axes, split_axis=0, concat_axis=0, tiled=True)]
    pallas_call x0 -> x1, Pallas kernels: none -> 18.5 us  [collect(): pl.pallas_call(lambda *refs: collect_kernel(planes, inner, *refs), in_spe...]
    all_to_all x1 -> x0, starting transfers between devices: 5.92 us -> none  [body(): lax.all_to_all(partial, axes, split_axis=0, concat_axis=0, tiled=True)]
    unnamed x56 -> x8, local copies, waits for them, and re-layouts: 4.47 us -> 0.02 us
    unnamed x14, other arithmetic: 4.26 us -> 8.42 us
    slice x4, local copies, waits for them, and re-layouts: 3.45 us -> 0.06 us  [half_tables(): ca, sa = (cos_c[:, a:a + 1], sin_c[:, a:a + 1])]
    dot_general x1, matrix products: 6.68 us -> 3.85 us  [body(): jnp.einsum('sbqi,bix->sbqx', weight_all, tile_mats, preferred_element_typ...]
    all_to_all x1, waiting for transfers between devices: 2.77 us -> 0.01 us  [body(): lax.all_to_all(weight_send, 'fault', split_axis=0, concat_axis=0, tiled=T...]
  transfers between devices with their start and end apart: 4 -> 3, of which waited for: 3 -> 2; matrix products, arithmetic and copies ran while one was open for 33% -> 37% of each run, Pallas kernels for 0% -> 0%
where the time goes in v4:
time: 89.3 us; the launch traced here: 88.6 us
  Pallas kernels  24.8 us (28%)
  other arithmetic  20.7 us (23%)
  local copies, waits for them, and re-layouts  15.9 us (18%)
  starting transfers between devices  15.2 us (17%)
  matrix products  6.81 us (8%)
  waiting for transfers between devices  4.25 us (5%)
  between operations  0.98 us (1%)
    pallas_call x1, Pallas kernels, collect(): pl.pallas_call(lambda *refs: collect_kernel(planes, inner, *refs), in_spe...  18.5 us
    reshape x1, local copies, waits for them, and re-layouts, body(): green.reshape(blocks_local, inner_width, comp_count * 2 * freq_local)  11.1 us
    unnamed x14, other arithmetic  8.42 us
    all_to_all x1, starting transfers between devices, body(): lax.all_to_all(weight_send, 'fault', split_axis=0, concat_axis=0, tiled=T...  7.39 us
    pallas_call x1, Pallas kernels, oscillate(): pl.pallas_call(oscillate_kernel, grid=(steps,), in_specs=[whole(spectra.s...  6.31 us
    all_to_all x1, starting transfers between devices, body(): lax.all_to_all(slip_send, axes, split_axis=0, concat_axis=0, tiled=True)  6.26 us
    dot_general x1, matrix products, body(): jnp.einsum('sbqi,bix->sbqx', weight_all, tile_mats, preferred_element_typ...  3.85 us
    ppermute x1, waiting for transfers between devices, body(): weight_recv.append(lax.ppermute(weight_own, 'rup', ring))  3.84 us
  transfers between devices with their start and end apart: 3, of which 2 were waited for; matrix products, arithmetic and copies ran while one was open for 37% of the time, Pallas kernels for 0%

profile of v4, /device:TPU:0, one launch (start us, length us, event | category | flops | bytes accessed | tf_op | source)
XLA Modules:
  0.0 88.6 jit_solution(6713710574624899132)
XLA Ops:
  0.7 1.0 %copy.31 = bf16[8,16,6,128]{3,2,1,0:T(8,128)(2,1)S(1)} copy(bf16[8,16,6,128]{3,1,2,0:T(8,128)(2,1)} %bitcast.126) | data formatting | bytes 393216 | tf_op jit(solution)/shard_map/transpose | solution.py:248
  1.8 0.8 fusion.104
  2.8 1.6 %convolution_convert_fusion.2 = bf16[256,768]{1,0:T(8,128)(2,1)} fusion(s32[768]{0:T(1024)S(1)} %fusion.97, bf16[16,8,6,128]{3,2,1,0:T(8,128)(2,1)S(1)} %bitcast.123, s32[128]{0:T(128)S(1)} %get-tuple-element.109, s32[128]{0:T(128)S(1)} %get-tuple-element.110, s32[256]{0:T(256)S(1)} %iota.116, s32[128]{0:T(128)S(1)} %eq.56, s32[256]{0:T(256)S(1)} %iota.113, ...), kind=kOutput, calls=%fused_computation.7 | convolution fusion | flops 202932224 | bytes 596608 | tf_op jit(solution)/shard_map/dot_general | solution.py:250
  4.4 7.4 %all-to-all-start = ((bf16[16,2,8,768]{3,2,1,0:T(8,128)(2,1)}), bf16[16,2,8,768]{3,2,1,0:T(8,128)(2,1)S(1)}, u32[]{:S(2)}, u32[]{:S(2)}) async-start(bf16[16,2,8,768]{3,2,1,0:T(8,128)(2,1)} %bitcast.1), calls=%async_computation | async-start | bytes 786432 | tf_op jit(solution)/shard_map/all_to_all | solution.py:252
  12.2 0.5 copy.34
  12.7 0.5 convolution_convert_fusion
  13.2 1.1 %sine_multiply_fusion.1 = (f32[512,128]{1,0:T(8,128)S(1)}, f32[512,128]{1,0:T(8,128)S(1)}) fusion(s32[512]{0:T(512)S(1)} %get-tuple-element.113), kind=kLoop, calls=%fused_computation.80 | loop fusion | flops 1048576 | bytes 526336 | tf_op jit(solution)/shard_map/mul | solution.py:30
  14.4 1.1 %sine_multiply_fusion = (f32[512,128]{1,0:T(8,128)S(1)}, f32[512,128]{1,0:T(8,128)S(1)}) fusion(s32[512]{0:T(512)S(1)} %get-tuple-element.114), kind=kLoop, calls=%fused_computation.68 | loop fusion | flops 1048576 | bytes 526336 | tf_op jit(solution)/shard_map/mul | solution.py:30
  18.0 0.9 %fusion.58 = (bf16[512,1024]{1,0:T(8,128)(2,1)}, bf16[512,1024]{1,0:T(8,128)(2,1)}) fusion(f32[512,128]{1,0:T(8,128)S(1)} %get-tuple-element.19, f32[512,128]{1,0:T(8,128)S(1)} %get-tuple-element.17, f32[512]{0:T(512)S(1)} %bitcast.142, f32[512]{0:T(512)S(1)} %bitcast.146), kind=kLoop, calls=%fused_computation.116 | loop fusion | flops 589822 | bytes 790528
  18.9 0.9 %fusion.59 = (bf16[512,1024]{1,0:T(8,128)(2,1)}, bf16[512,1024]{1,0:T(8,128)(2,1)}) fusion(bf16[512,1024]{1,0:T(8,128)(2,1)} %get-tuple-element.42, f32[512,128]{1,0:T(8,128)S(1)} %get-tuple-element.19, f32[512,128]{1,0:T(8,128)S(1)} %get-tuple-element.17, f32[512]{0:T(512)S(1)} %bitcast.140, f32[512]{0:T(512)S(1)} %bitcast.145, ...), kind=kLoop, calls=%fused_computation.117 | loop fusion | flops 589824 | bytes 790528
  19.8 1.0 %fusion.60 = (bf16[512,1024]{1,0:T(8,128)(2,1)}, bf16[512,1024]{1,0:T(8,128)(2,1)}) fusion(bf16[512,1024]{1,0:T(8,128)(2,1)} %get-tuple-element.40, f32[512,128]{1,0:T(8,128)S(1)} %get-tuple-element.19, f32[512,128]{1,0:T(8,128)S(1)} %get-tuple-element.17, f32[512]{0:T(512)S(1)} %bitcast.138, f32[512]{0:T(512)S(1)} %bitcast.141, ...), kind=kLoop, calls=%fused_computation.118 | loop fusion | flops 589824 | bytes 790528
  20.8 1.1 %copy.35 = bf16[16,2,2,2,8,512]{5,4,2,3,1,0:T(8,128)(2,1)} copy(bf16[16,2,2,2,8,512]{5,4,3,1,2,0:T(8,128)(2,1)S(1)} %bitcast.114) | data formatting | bytes 2097152 | tf_op jit(solution)/shard_map/transpose | solution.py:263
  21.9 1.0 %fusion.61 = (bf16[512,1024]{1,0:T(8,128)(2,1)}, bf16[512,1024]{1,0:T(8,128)(2,1)}) fusion(bf16[512,1024]{1,0:T(8,128)(2,1)} %get-tuple-element.38, f32[512,128]{1,0:T(8,128)S(1)} %get-tuple-element.19, f32[512,128]{1,0:T(8,128)S(1)} %get-tuple-element.17, f32[512]{0:T(512)S(1)} %bitcast.135, f32[512]{0:T(512)S(1)} %bitcast.137, ...), kind=kLoop, calls=%fused_computation.119 | loop fusion | flops 589824 | bytes 790528
  22.9 1.0 %fusion.62 = (bf16[512,1024]{1,0:T(8,128)(2,1)}, bf16[512,1024]{1,0:T(8,128)(2,1)}) fusion(bf16[512,1024]{1,0:T(8,128)(2,1)} %get-tuple-element.36, f32[512,128]{1,0:T(8,128)S(1)} %get-tuple-element.19, f32[512,128]{1,0:T(8,128)S(1)} %get-tuple-element.17, f32[512]{0:T(512)S(1)} %bitcast.133, f32[512]{0:T(512)S(1)} %bitcast.136, ...), kind=kLoop, calls=%fused_computation.120 | loop fusion | flops 589824 | bytes 790528
  23.8 0.9 %fusion.63 = (bf16[512,1024]{1,0:T(8,128)(2,1)}, bf16[512,1024]{1,0:T(8,128)(2,1)}) fusion(bf16[512,1024]{1,0:T(8,128)(2,1)} %get-tuple-element.34, f32[512,128]{1,0:T(8,128)S(1)} %get-tuple-element.19, f32[512,128]{1,0:T(8,128)S(1)} %get-tuple-element.17, f32[512]{0:T(512)S(1)} %bitcast.132, f32[512]{0:T(512)S(1)} %bitcast.134, ...), kind=kLoop, calls=%fused_computation.121 | loop fusion | flops 589824 | bytes 790528
  24.8 6.3 %all-to-all-start.1 = ((bf16[32,2,2,8,512]{4,3,1,2,0:T(8,128)(2,1)}), bf16[32,2,2,8,512]{4,3,1,2,0:T(8,128)(2,1)}, u32[]{:S(2)}, u32[]{:S(2)}) async-start(bf16[32,2,2,8,512]{4,3,1,2,0:T(8,128)(2,1)} %bitcast.115), calls=%async_computation.1 | async-start | bytes 2097152 | tf_op jit(solution)/shard_map/all_to_all | solution.py:265
  31.0 1.0 %fusion.15 = (f32[1,2,64,512]{3,2,1,0:T(8,128)}, f32[1,2,64,512]{3,2,1,0:T(8,128)}) fusion(f32[2,512]{1,0:T(2,128)S(1)} %get-tuple-element.111, f32[64]{0:T(128)S(1)} %get-tuple-element.108, f32[2,512]{1,0:T(2,128)S(1)} %get-tuple-element.112, f32[64]{0:T(128)S(1)} %get-tuple-element.106, f32[64]{0:T(128)S(1)} %get-tuple-element.107), kind=kLoop, calls=%fused_computation.35 | loop fusion | flops 589824 | bytes 533248 | tf_op jit(solution)/shard_map/div | solution.py:52
  32.0 0.9 %fusion.64 = (bf16[512,1024]{1,0:T(8,128)(2,1)}, bf16[512,1024]{1,0:T(8,128)(2,1)}) fusion(bf16[512,1024]{1,0:T(8,128)(2,1)} %get-tuple-element.32, f32[512,128]{1,0:T(8,128)S(1)} %get-tuple-element.19, f32[512,128]{1,0:T(8,128)S(1)} %get-tuple-element.17, f32[512]{0:T(512)S(1)} %bitcast.130, f32[512]{0:T(512)S(1)} %bitcast.131, ...), kind=kLoop, calls=%fused_computation.122 | loop fusion | flops 589824 | bytes 790528
  32.9 1.5 %collective-permute-start = (bf16[16,2,8,768]{3,2,1,0:T(8,128)(2,1)S(1)}, bf16[16,2,8,768]{3,2,1,0:T(8,128)(2,1)}, u32[]{:S(2)}, u32[]{:S(2)}) collective-permute-start(bf16[16,2,8,768]{3,2,1,0:T(8,128)(2,1)S(1)} %all-to-all-done), channel_id=1, source_target_pairs={{0,1},{1,0},{2,3},{3,2},{4,5},{5,4},{6,7},{7,6},{8,9},{9,8},{10,11... | collective-permute-start | bytes 1179656 | tf_op jit(solution)/shard_map/ppermute | solution.py:257
  34.4 11.1 %reshape.231 = bf16[2,768,2048,1]{2,1,0,3:T(8,128)(2,1)} reshape(bf16[2,128,6,2,2,512]{5,4,3,2,1,0:T(2,128)(2,1)} %param.7) | data formatting | bytes 12582912 | tf_op jit(solution)/shard_map/reshape | solution.py:266
  45.6 1.2 %pad_maximum_fusion.2.gain_ref = f32[2,2,64,512]{3,2,1,0:T(8,128)S(1)} fusion(f32[1,2,64,512]{3,2,1,0:T(8,128)} %get-tuple-element.95, f32[1,2,64,512]{3,2,1,0:T(8,128)} %get-tuple-element.94), kind=kLoop, calls=%fused_computation.21 | loop fusion | flops 131072 | bytes 1048576 | tf_op jit(solution)/shard_map/concatenate | solution.py:51
  46.8 0.9 %fusion.65 = (bf16[512,1024]{1,0:T(8,128)(2,1)}, bf16[512,1024]{1,0:T(8,128)(2,1)}) fusion(bf16[512,1024]{1,0:T(8,128)(2,1)} %get-tuple-element.30, f32[512,128]{1,0:T(8,128)S(1)} %get-tuple-element.19, f32[512,128]{1,0:T(8,128)S(1)} %get-tuple-element.17, f32[512]{0:T(512)S(1)} %bitcast.128, f32[512]{0:T(512)S(1)} %bitcast.129, ...), kind=kLoop, calls=%fused_computation.123 | loop fusion | flops 589824 | bytes 790528 | tf_op jit(solution)/shard_map/concatenate | solution.py:38
  47.7 3.8 %collective-permute-done = bf16[16,2,8,768]{3,2,1,0:T(8,128)(2,1)} collective-permute-done((bf16[16,2,8,768]{3,2,1,0:T(8,128)(2,1)S(1)}, bf16[16,2,8,768]{3,2,1,0:T(8,128)(2,1)}, u32[]{:S(2)}, u32[]{:S(2)}) %collective-permute-start) | collective-permute-done | bytes 393248 | tf_op jit(solution)/shard_map/ppermute | solution.py:257
  51.6 1.1 %select_bitcast_fusion.1 = (bf16[16,1,2,8,768]{4,3,2,0,1:T(8,128)(2,1)S(1)}, bf16[16,1,2,8,768]{4,3,2,0,1:T(8,128)(2,1)S(1)}) fusion(bf16[16,2,8,768]{3,2,1,0:T(8,128)(2,1)S(1)} %all-to-all-done, bf16[16,2,8,768]{3,2,1,0:T(8,128)(2,1)} %collective-permute-done, pred[]{:T(512)S(6)} %select_n.126, pred[]{:T(512)S(6)} %select_n.135), kind=kLoop, calls=%fused_computation.30 | loop fusion | flops 393216 | bytes 1572866 | tf_op jit(solution)/shard_map/stack | solution.py:267
  52.8 3.9 %fusion.2 = f32[32,2,8,2048]{3,2,0,1:T(8,128)} fusion(bf16[32,2,8,768]{3,2,0,1:T(8,128)(2,1)S(1)} %bitcast.113, bf16[2,768,2048,1]{2,1,0,3:T(8,128)(2,1)S(1)} %copy-done), kind=kOutput, calls=%fused_computation.2 | convolution fusion | flops 1610612736 | bytes 11272192 | tf_op jit(solution)/shard_map/sbqi,bix->sbqx/dot_general | solution.py:278
  57.0 1.5 %copy_convert_fusion = f32[32,2,2,8,512]{4,3,0,1,2:T(8,128)S(1)} fusion(bf16[32,2,2,8,512]{4,3,1,2,0:T(8,128)(2,1)} %all-to-all-done.1), kind=kLoop, calls=%fused_computation.14 | loop fusion | flops 524288 | bytes 3145728 | tf_op jit(solution)/shard_map/convert_element_type | solution.py:279
  58.5 2.8 %subtract_reduce_fusion.1 = (bf16[32,8,512]{2,1,0:T(8,128)(2,1)S(1)}, bf16[32,8,512]{2,1,0:T(8,128)(2,1)S(1)}, bf16[32,8,512]{2,1,0:T(8,128)(2,1)S(1)}, bf16[32,8,512]{2,1,0:T(8,128)(2,1)S(1)}) fusion(f32[32,2,8,2048]{3,2,0,1:T(8,128)} %fusion.2, f32[32,2,2,8,512]{4,3,0,1,2:T(8,128)S(1)} %copy_convert_fusion), kind=kLoop, calls=%fused_computation.19 | loop fusion | flops 3670016 | bytes 7340032 | tf_op jit(solution)/shard_map/reduce_sum | solution.py:286
  61.5 0.8 convolution_convert_fusion.1
  62.3 18.5 %shard_map.86 = f32[2,32,512]{2,1,0:T(8,128)S(1)} custom-call(bf16[4,8,32,512]{3,2,1,0:T(8,128)(2,1)S(1)} %bitcast.109), custom_call_target="tpu_custom_call" | custom-call | tf_op jit(solution)/shard_map/pallas_call | solution.py:205
  80.9 6.3 %shard_map.87 = (f32[16,2048]{1,0:T(8,128)S(1)}, f32[4,4,64]{2,1,0:T(4,128)S(1)}) custom-call(f32[2,2,16,512]{3,2,1,0:T(8,128)S(1)} %bitcast.110, f32[2,2,64,512]{3,2,1,0:T(8,128)S(1)} %pad_maximum_fusion.2.gain_ref, bf16[512,1024]{1,0:T(8,128)(2,1)S(1)} %get-tuple-element.45.ce_ref, bf16[512,1024]{1,0:T(8,128)(2,1)} %get-tuple-element.29.co_ref, ...), custom_call_target="tpu_custom_call" | custom-call | tf_op jit(solution)/shard_map/pallas_call | solution.py:110
  87.2 0.8 copy.54
  88.0 0.6 copy.55
  (43 shorter events, 3.7 us)
Async XLA Ops:
  0.6 11.2 %copy-start.1 = (bf16[8,16,2,1024]{3,2,1,0:T(2,128)(2,1)S(1)}, bf16[8,16,2,1024]{3,2,1,0:T(2,128)(2,1)}, u32[]{:S(2)}) copy-start(bf16[8,16,2,1024]{3,2,1,0:T(2,128)(2,1)} %param.9) | copy-start | bytes 1572868
  4.4 20.3 %all-to-all-start = ((bf16[16,2,8,768]{3,2,1,0:T(8,128)(2,1)}), bf16[16,2,8,768]{3,2,1,0:T(8,128)(2,1)S(1)}, u32[]{:S(2)}, u32[]{:S(2)}) async-start(bf16[16,2,8,768]{3,2,1,0:T(8,128)(2,1)} %bitcast.1), calls=%async_computation | async-start | bytes 786432 | tf_op jit(solution)/shard_map/all_to_all | solution.py:252
  11.8 4.0 %copy-start.2 = (f32[64]{0:T(128)S(1)}, f32[64]{0:T(128)}, u32[]{:S(2)}) copy-start(f32[64]{0:T(128)} %param.12) | copy-start | bytes 772
  11.8 4.0 %copy-start.3 = (f32[64]{0:T(128)S(1)}, f32[64]{0:T(128)}, u32[]{:S(2)}) copy-start(f32[64]{0:T(128)} %param.13) | copy-start | bytes 772
  24.8 32.3 %all-to-all-start.1 = ((bf16[32,2,2,8,512]{4,3,1,2,0:T(8,128)(2,1)}), bf16[32,2,2,8,512]{4,3,1,2,0:T(8,128)(2,1)}, u32[]{:S(2)}, u32[]{:S(2)}) async-start(bf16[32,2,2,8,512]{4,3,1,2,0:T(8,128)(2,1)} %bitcast.115), calls=%async_computation.1 | async-start | bytes 2097152 | tf_op jit(solution)/shard_map/all_to_all | solution.py:265
  32.9 18.6 %collective-permute-start = (bf16[16,2,8,768]{3,2,1,0:T(8,128)(2,1)S(1)}, bf16[16,2,8,768]{3,2,1,0:T(8,128)(2,1)}, u32[]{:S(2)}, u32[]{:S(2)}) collective-permute-start(bf16[16,2,8,768]{3,2,1,0:T(8,128)(2,1)S(1)} %all-to-all-done), channel_id=1, source_target_pairs={{0,1},{1,0},{2,3},{3,2},{4,5},{5,4},{6,7},{7,6},{8,9},{9,8},{10,11... | collective-permute-start | bytes 1179656 | tf_op jit(solution)/shard_map/ppermute | solution.py:257
  45.6 7.2 %copy-start = (bf16[2,768,2048,1]{2,1,0,3:T(8,128)(2,1)S(1)}, bf16[2,768,2048,1]{2,1,0,3:T(8,128)(2,1)}, u32[]{:S(2)}) copy-start(bf16[2,768,2048,1]{2,1,0,3:T(8,128)(2,1)} %reshape.231) | copy-start | bytes 18874372

commit v5 on v4

--- a/solution.py
+++ b/solution.py
@@ -104,7 +104,7 @@
 def oscillate(spectra, gain, tables):
     row_count, half = spectra.shape[2:]
     period_count = gain.shape[2]
-    rows_per = math.gcd(row_count, 4)
+    rows_per = math.gcd(row_count, 8)
     steps = row_count // rows_per
     whole = lambda shape: pl.BlockSpec(shape, lambda i: (0,) * len(shape), pipeline_mode=pl.Buffered(1))
     wave, peak = pl.pallas_call(

time: 89.3 us -> 88.9 us (level)
  no operation moved by 1% of the time
where the time goes in v5:
time: 88.9 us; the launch traced here: 88.2 us
  Pallas kernels  24.4 us (27%)
  other arithmetic  20.7 us (23%)
  local copies, waits for them, and re-layouts  15.9 us (18%)
  starting transfers between devices  15.2 us (17%)
  matrix products  6.81 us (8%)
  waiting for transfers between devices  4.25 us (5%)
  between operations  0.98 us (1%)
    pallas_call x1, Pallas kernels, collect(): pl.pallas_call(lambda *refs: collect_kernel(planes, inner, *refs), in_spe...  18.5 us
    reshape x1, local copies, waits for them, and re-layouts, body(): green.reshape(blocks_local, inner_width, comp_count * 2 * freq_local)  11.1 us
    unnamed x14, other arithmetic  8.42 us
    all_to_all x1, starting transfers between devices, body(): lax.all_to_all(weight_send, 'fault', split_axis=0, concat_axis=0, tiled=T...  7.39 us
    all_to_all x1, starting transfers between devices, body(): lax.all_to_all(slip_send, axes, split_axis=0, concat_axis=0, tiled=True)  6.26 us
    pallas_call x1, Pallas kernels, oscillate(): pl.pallas_call(oscillate_kernel, grid=(steps,), in_specs=[whole(spectra.s...  5.87 us
    dot_general x1, matrix products, body(): jnp.einsum('sbqi,bix->sbqx', weight_all, tile_mats, preferred_element_typ...  3.85 us
    ppermute x1, waiting for transfers between devices, body(): weight_recv.append(lax.ppermute(weight_own, 'rup', ring))  3.84 us
  transfers between devices with their start and end apart: 3, of which 2 were waited for; matrix products, arithmetic and copies ran while one was open for 37% of the time, Pallas kernels for 0%

profile of v5, /device:TPU:0, one launch (start us, length us, event | category | flops | bytes accessed | tf_op | source)
XLA Modules:
  0.0 88.2 jit_solution(4920988607435655368)
XLA Ops:
  0.7 1.0 %copy.31 = bf16[8,16,6,128]{3,2,1,0:T(8,128)(2,1)S(1)} copy(bf16[8,16,6,128]{3,1,2,0:T(8,128)(2,1)} %bitcast.123) | data formatting | bytes 393216 | tf_op jit(solution)/shard_map/transpose | solution.py:248
  1.8 0.8 fusion.104
  2.8 1.6 %convolution_convert_fusion.2 = bf16[256,768]{1,0:T(8,128)(2,1)} fusion(s32[768]{0:T(1024)S(1)} %fusion.97, bf16[16,8,6,128]{3,2,1,0:T(8,128)(2,1)S(1)} %bitcast.120, s32[128]{0:T(128)S(1)} %get-tuple-element.119, s32[128]{0:T(128)S(1)} %get-tuple-element.120, s32[256]{0:T(256)S(1)} %iota.116, s32[128]{0:T(128)S(1)} %eq.56, s32[256]{0:T(256)S(1)} %iota.113, ...), kind=kOutput, calls=%fused_computation.7 | convolution fusion | flops 202932224 | bytes 596608 | tf_op jit(solution)/shard_map/dot_general | solution.py:250
  4.4 7.4 %all-to-all-start = ((bf16[16,2,8,768]{3,2,1,0:T(8,128)(2,1)}), bf16[16,2,8,768]{3,2,1,0:T(8,128)(2,1)S(1)}, u32[]{:S(2)}, u32[]{:S(2)}) async-start(bf16[16,2,8,768]{3,2,1,0:T(8,128)(2,1)} %bitcast.1), calls=%async_computation | async-start | bytes 786432 | tf_op jit(solution)/shard_map/all_to_all | solution.py:252
  12.2 0.5 copy.34
  12.7 0.5 convolution_convert_fusion
  13.2 1.1 %sine_multiply_fusion.1 = (f32[512,128]{1,0:T(8,128)S(1)}, f32[512,128]{1,0:T(8,128)S(1)}) fusion(s32[512]{0:T(512)S(1)} %get-tuple-element.117), kind=kLoop, calls=%fused_computation.80 | loop fusion | flops 1048576 | bytes 526336 | tf_op jit(solution)/shard_map/mul | solution.py:30
  14.4 1.1 %sine_multiply_fusion = (f32[512,128]{1,0:T(8,128)S(1)}, f32[512,128]{1,0:T(8,128)S(1)}) fusion(s32[512]{0:T(512)S(1)} %get-tuple-element.118), kind=kLoop, calls=%fused_computation.68 | loop fusion | flops 1048576 | bytes 526336 | tf_op jit(solution)/shard_map/mul | solution.py:30
  18.0 0.9 %fusion.58 = (bf16[512,1024]{1,0:T(8,128)(2,1)}, bf16[512,1024]{1,0:T(8,128)(2,1)}) fusion(f32[512,128]{1,0:T(8,128)S(1)} %get-tuple-element.19, f32[512,128]{1,0:T(8,128)S(1)} %get-tuple-element.17, f32[512]{0:T(512)S(1)} %bitcast.139, f32[512]{0:T(512)S(1)} %bitcast.143), kind=kLoop, calls=%fused_computation.116 | loop fusion | flops 589822 | bytes 790528
  18.9 0.9 %fusion.59 = (bf16[512,1024]{1,0:T(8,128)(2,1)}, bf16[512,1024]{1,0:T(8,128)(2,1)}) fusion(bf16[512,1024]{1,0:T(8,128)(2,1)} %get-tuple-element.50, f32[512,128]{1,0:T(8,128)S(1)} %get-tuple-element.19, f32[512,128]{1,0:T(8,128)S(1)} %get-tuple-element.17, f32[512]{0:T(512)S(1)} %bitcast.137, f32[512]{0:T(512)S(1)} %bitcast.142, ...), kind=kLoop, calls=%fused_computation.117 | loop fusion | flops 589824 | bytes 790528
  19.8 1.0 %fusion.60 = (bf16[512,1024]{1,0:T(8,128)(2,1)}, bf16[512,1024]{1,0:T(8,128)(2,1)}) fusion(bf16[512,1024]{1,0:T(8,128)(2,1)} %get-tuple-element.48, f32[512,128]{1,0:T(8,128)S(1)} %get-tuple-element.19, f32[512,128]{1,0:T(8,128)S(1)} %get-tuple-element.17, f32[512]{0:T(512)S(1)} %bitcast.135, f32[512]{0:T(512)S(1)} %bitcast.138, ...), kind=kLoop, calls=%fused_computation.118 | loop fusion | flops 589824 | bytes 790528
  20.8 1.1 %copy.35 = bf16[16,2,2,2,8,512]{5,4,2,3,1,0:T(8,128)(2,1)} copy(bf16[16,2,2,2,8,512]{5,4,3,1,2,0:T(8,128)(2,1)S(1)} %bitcast.111) | data formatting | bytes 2097152 | tf_op jit(solution)/shard_map/transpose | solution.py:263
  21.9 1.0 %fusion.61 = (bf16[512,1024]{1,0:T(8,128)(2,1)}, bf16[512,1024]{1,0:T(8,128)(2,1)}) fusion(bf16[512,1024]{1,0:T(8,128)(2,1)} %get-tuple-element.46, f32[512,128]{1,0:T(8,128)S(1)} %get-tuple-element.19, f32[512,128]{1,0:T(8,128)S(1)} %get-tuple-element.17, f32[512]{0:T(512)S(1)} %bitcast.132, f32[512]{0:T(512)S(1)} %bitcast.134, ...), kind=kLoop, calls=%fused_computation.119 | loop fusion | flops 589824 | bytes 790528
  22.9 1.0 %fusion.62 = (bf16[512,1024]{1,0:T(8,128)(2,1)}, bf16[512,1024]{1,0:T(8,128)(2,1)}) fusion(bf16[512,1024]{1,0:T(8,128)(2,1)} %get-tuple-element.44, f32[512,128]{1,0:T(8,128)S(1)} %get-tuple-element.19, f32[512,128]{1,0:T(8,128)S(1)} %get-tuple-element.17, f32[512]{0:T(512)S(1)} %bitcast.130, f32[512]{0:T(512)S(1)} %bitcast.133, ...), kind=kLoop, calls=%fused_computation.120 | loop fusion | flops 589824 | bytes 790528
  23.8 0.9 %fusion.63 = (bf16[512,1024]{1,0:T(8,128)(2,1)}, bf16[512,1024]{1,0:T(8,128)(2,1)}) fusion(bf16[512,1024]{1,0:T(8,128)(2,1)} %get-tuple-element.42, f32[512,128]{1,0:T(8,128)S(1)} %get-tuple-element.19, f32[512,128]{1,0:T(8,128)S(1)} %get-tuple-element.17, f32[512]{0:T(512)S(1)} %bitcast.129, f32[512]{0:T(512)S(1)} %bitcast.131, ...), kind=kLoop, calls=%fused_computation.121 | loop fusion | flops 589824 | bytes 790528
  24.8 6.3 %all-to-all-start.1 = ((bf16[32,2,2,8,512]{4,3,1,2,0:T(8,128)(2,1)}), bf16[32,2,2,8,512]{4,3,1,2,0:T(8,128)(2,1)}, u32[]{:S(2)}, u32[]{:S(2)}) async-start(bf16[32,2,2,8,512]{4,3,1,2,0:T(8,128)(2,1)} %bitcast.112), calls=%async_computation.1 | async-start | bytes 2097152 | tf_op jit(solution)/shard_map/all_to_all | solution.py:265
  31.0 1.0 %fusion.15 = (f32[1,2,64,512]{3,2,1,0:T(8,128)}, f32[1,2,64,512]{3,2,1,0:T(8,128)}) fusion(f32[2,512]{1,0:T(2,128)S(1)} %get-tuple-element.121, f32[64]{0:T(128)S(1)} %get-tuple-element.116, f32[2,512]{1,0:T(2,128)S(1)} %get-tuple-element.122, f32[64]{0:T(128)S(1)} %get-tuple-element.114, f32[64]{0:T(128)S(1)} %get-tuple-element.115), kind=kLoop, calls=%fused_computation.35 | loop fusion | flops 589824 | bytes 533248 | tf_op jit(solution)/shard_map/div | solution.py:52
  32.0 0.9 %fusion.64 = (bf16[512,1024]{1,0:T(8,128)(2,1)}, bf16[512,1024]{1,0:T(8,128)(2,1)}) fusion(bf16[512,1024]{1,0:T(8,128)(2,1)} %get-tuple-element.40, f32[512,128]{1,0:T(8,128)S(1)} %get-tuple-element.19, f32[512,128]{1,0:T(8,128)S(1)} %get-tuple-element.17, f32[512]{0:T(512)S(1)} %bitcast.127, f32[512]{0:T(512)S(1)} %bitcast.128, ...), kind=kLoop, calls=%fused_computation.122 | loop fusion | flops 589824 | bytes 790528
  32.9 1.5 %collective-permute-start = (bf16[16,2,8,768]{3,2,1,0:T(8,128)(2,1)S(1)}, bf16[16,2,8,768]{3,2,1,0:T(8,128)(2,1)}, u32[]{:S(2)}, u32[]{:S(2)}) collective-permute-start(bf16[16,2,8,768]{3,2,1,0:T(8,128)(2,1)S(1)} %all-to-all-done), channel_id=1, source_target_pairs={{0,1},{1,0},{2,3},{3,2},{4,5},{5,4},{6,7},{7,6},{8,9},{9,8},{10,11... | collective-permute-start | bytes 1179656 | tf_op jit(solution)/shard_map/ppermute | solution.py:257
  34.4 11.1 %reshape.227 = bf16[2,768,2048,1]{2,1,0,3:T(8,128)(2,1)} reshape(bf16[2,128,6,2,2,512]{5,4,3,2,1,0:T(2,128)(2,1)} %param.7) | data formatting | bytes 12582912 | tf_op jit(solution)/shard_map/reshape | solution.py:266
  45.6 1.2 %pad_maximum_fusion.2.gain_ref = f32[2,2,64,512]{3,2,1,0:T(8,128)S(1)} fusion(f32[1,2,64,512]{3,2,1,0:T(8,128)} %get-tuple-element.103, f32[1,2,64,512]{3,2,1,0:T(8,128)} %get-tuple-element.102), kind=kLoop, calls=%fused_computation.21 | loop fusion | flops 131072 | bytes 1048576 | tf_op jit(solution)/shard_map/concatenate | solution.py:51
  46.8 0.9 %fusion.65 = (bf16[512,1024]{1,0:T(8,128)(2,1)}, bf16[512,1024]{1,0:T(8,128)(2,1)}) fusion(bf16[512,1024]{1,0:T(8,128)(2,1)} %get-tuple-element.38, f32[512,128]{1,0:T(8,128)S(1)} %get-tuple-element.19, f32[512,128]{1,0:T(8,128)S(1)} %get-tuple-element.17, f32[512]{0:T(512)S(1)} %bitcast.125, f32[512]{0:T(512)S(1)} %bitcast.126, ...), kind=kLoop, calls=%fused_computation.123 | loop fusion | flops 589824 | bytes 790528 | tf_op jit(solution)/shard_map/concatenate | solution.py:38
  47.7 3.8 %collective-permute-done = bf16[16,2,8,768]{3,2,1,0:T(8,128)(2,1)} collective-permute-done((bf16[16,2,8,768]{3,2,1,0:T(8,128)(2,1)S(1)}, bf16[16,2,8,768]{3,2,1,0:T(8,128)(2,1)}, u32[]{:S(2)}, u32[]{:S(2)}) %collective-permute-start) | collective-permute-done | bytes 393248 | tf_op jit(solution)/shard_map/ppermute | solution.py:257
  51.6 1.1 %select_bitcast_fusion.1 = (bf16[16,1,2,8,768]{4,3,2,0,1:T(8,128)(2,1)S(1)}, bf16[16,1,2,8,768]{4,3,2,0,1:T(8,128)(2,1)S(1)}) fusion(bf16[16,2,8,768]{3,2,1,0:T(8,128)(2,1)S(1)} %all-to-all-done, bf16[16,2,8,768]{3,2,1,0:T(8,128)(2,1)} %collective-permute-done, pred[]{:T(512)S(6)} %select_n.126, pred[]{:T(512)S(6)} %select_n.135), kind=kLoop, calls=%fused_computation.30 | loop fusion | flops 393216 | bytes 1572866 | tf_op jit(solution)/shard_map/stack | solution.py:267
  52.8 3.9 %fusion.2 = f32[32,2,8,2048]{3,2,0,1:T(8,128)} fusion(bf16[32,2,8,768]{3,2,0,1:T(8,128)(2,1)S(1)} %bitcast.110, bf16[2,768,2048,1]{2,1,0,3:T(8,128)(2,1)S(1)} %copy-done), kind=kOutput, calls=%fused_computation.2 | convolution fusion | flops 1610612736 | bytes 11272192 | tf_op jit(solution)/shard_map/sbqi,bix->sbqx/dot_general | solution.py:278
  57.0 1.5 %copy_convert_fusion = f32[32,2,2,8,512]{4,3,0,1,2:T(8,128)S(1)} fusion(bf16[32,2,2,8,512]{4,3,1,2,0:T(8,128)(2,1)} %all-to-all-done.1), kind=kLoop, calls=%fused_computation.14 | loop fusion | flops 524288 | bytes 3145728 | tf_op jit(solution)/shard_map/convert_element_type | solution.py:279
  58.5 2.8 %subtract_reduce_fusion.1 = (bf16[32,8,512]{2,1,0:T(8,128)(2,1)S(1)}, bf16[32,8,512]{2,1,0:T(8,128)(2,1)S(1)}, bf16[32,8,512]{2,1,0:T(8,128)(2,1)S(1)}, bf16[32,8,512]{2,1,0:T(8,128)(2,1)S(1)}) fusion(f32[32,2,8,2048]{3,2,0,1:T(8,128)} %fusion.2, f32[32,2,2,8,512]{4,3,0,1,2:T(8,128)S(1)} %copy_convert_fusion), kind=kLoop, calls=%fused_computation.19 | loop fusion | flops 3670016 | bytes 7340032 | tf_op jit(solution)/shard_map/reduce_sum | solution.py:286
  61.5 0.8 convolution_convert_fusion.1
  62.3 18.5 %shard_map.86 = f32[2,32,512]{2,1,0:T(8,128)S(1)} custom-call(bf16[4,8,32,512]{3,2,1,0:T(8,128)(2,1)S(1)} %bitcast.106), custom_call_target="tpu_custom_call" | custom-call | tf_op jit(solution)/shard_map/pallas_call | solution.py:205
  80.9 5.9 %shard_map.87 = (f32[16,2048]{1,0:T(8,128)S(1)}, f32[2,8,64]{2,1,0:T(8,128)S(1)}) custom-call(f32[2,2,16,512]{3,2,1,0:T(8,128)S(1)} %bitcast.107, f32[2,2,64,512]{3,2,1,0:T(8,128)S(1)} %pad_maximum_fusion.2.gain_ref, bf16[512,1024]{1,0:T(8,128)(2,1)S(1)} %get-tuple-element.53.ce_ref, bf16[512,1024]{1,0:T(8,128)(2,1)} %get-tuple-element.37.co_ref, ...), custom_call_target="tpu_custom_call" | custom-call | tf_op jit(solution)/shard_map/pallas_call | solution.py:110
  86.8 0.8 copy.53
  87.5 0.6 copy.40
  (43 shorter events, 3.7 us)
Async XLA Ops:
  0.6 11.2 %copy-start.1 = (bf16[8,16,2,1024]{3,2,1,0:T(2,128)(2,1)S(1)}, bf16[8,16,2,1024]{3,2,1,0:T(2,128)(2,1)}, u32[]{:S(2)}) copy-start(bf16[8,16,2,1024]{3,2,1,0:T(2,128)(2,1)} %param.9) | copy-start | bytes 1572868
  4.4 20.3 %all-to-all-start = ((bf16[16,2,8,768]{3,2,1,0:T(8,128)(2,1)}), bf16[16,2,8,768]{3,2,1,0:T(8,128)(2,1)S(1)}, u32[]{:S(2)}, u32[]{:S(2)}) async-start(bf16[16,2,8,768]{3,2,1,0:T(8,128)(2,1)} %bitcast.1), calls=%async_computation | async-start | bytes 786432 | tf_op jit(solution)/shard_map/all_to_all | solution.py:252
  11.8 4.0 %copy-start.2 = (f32[64]{0:T(128)S(1)}, f32[64]{0:T(128)}, u32[]{:S(2)}) copy-start(f32[64]{0:T(128)} %param.12) | copy-start | bytes 772
  11.8 4.0 %copy-start.3 = (f32[64]{0:T(128)S(1)}, f32[64]{0:T(128)}, u32[]{:S(2)}) copy-start(f32[64]{0:T(128)} %param.13) | copy-start | bytes 772
  24.8 32.3 %all-to-all-start.1 = ((bf16[32,2,2,8,512]{4,3,1,2,0:T(8,128)(2,1)}), bf16[32,2,2,8,512]{4,3,1,2,0:T(8,128)(2,1)}, u32[]{:S(2)}, u32[]{:S(2)}) async-start(bf16[32,2,2,8,512]{4,3,1,2,0:T(8,128)(2,1)} %bitcast.112), calls=%async_computation.1 | async-start | bytes 2097152 | tf_op jit(solution)/shard_map/all_to_all | solution.py:265
  32.9 18.6 %collective-permute-start = (bf16[16,2,8,768]{3,2,1,0:T(8,128)(2,1)S(1)}, bf16[16,2,8,768]{3,2,1,0:T(8,128)(2,1)}, u32[]{:S(2)}, u32[]{:S(2)}) collective-permute-start(bf16[16,2,8,768]{3,2,1,0:T(8,128)(2,1)S(1)} %all-to-all-done), channel_id=1, source_target_pairs={{0,1},{1,0},{2,3},{3,2},{4,5},{5,4},{6,7},{7,6},{8,9},{9,8},{10,11... | collective-permute-start | bytes 1179656 | tf_op jit(solution)/shard_map/ppermute | solution.py:257
  45.6 7.2 %copy-start = (bf16[2,768,2048,1]{2,1,0,3:T(8,128)(2,1)S(1)}, bf16[2,768,2048,1]{2,1,0,3:T(8,128)(2,1)}, u32[]{:S(2)}) copy-start(bf16[2,768,2048,1]{2,1,0,3:T(8,128)(2,1)} %reshape.227) | copy-start | bytes 18874372
